TPU v7x, 32 devices: a whole 2x2x4 slice. The times are simulated.
32 devices in a mesh: dp: 2 (over core), fsdp: 16 (over z, y, x).
Axes of the slice: x: 2, y: 2, z: 4, core: 2. Of those that a mesh axis runs over, the one named last changes fastest.
Arguments:
- hidden: bfloat16 [32768, 768], P(('dp', 'fsdp')), may hold values from -6 to 6
- gain_attn: bfloat16 [768], P('fsdp'), may hold values from 0.5 to 1.5
- rel_table: bfloat16 [384], P('fsdp'), may hold values from -4 to 4
- query_weight: bfloat16 [768, 768], P('fsdp'), may hold values from -0.0546875 to 0.0546875
- key_weight: bfloat16 [768, 768], P('fsdp'), may hold values from -0.21875 to 0.21875
- value_weight: bfloat16 [768, 768], P('fsdp'), may hold values from -0.21875 to 0.21875
- output_weight: bfloat16 [768, 768], P('fsdp'), may hold values from -0.625 to 0.625
- gain_ffn: bfloat16 [768], P('fsdp'), may hold values from 0.5 to 1.5
- inner_weight: bfloat16 [768, 3072], P('fsdp'), may hold values from -0.21875 to 0.21875
- outer_weight: bfloat16 [3072, 768], P('fsdp'), may hold values from -0.109375 to 0.109375
- lengths: int32 [160], P(('dp', 'fsdp')), may hold values from 33 to 512, as said below
- cotangent: bfloat16 [32768, 768], P(('dp', 'fsdp')), may hold values from -6 to 6
Outputs:
- result: float32 [32768, 768], P(('dp', 'fsdp'))
- grad_hidden: float32 [32768, 768], P(('dp', 'fsdp'))
- grad_gain_attn: float32 [768], P('fsdp')
- grad_rel_table: float32 [384], P('fsdp')
- grad_query_weight: float32 [768, 768], P('fsdp')
- grad_key_weight: float32 [768, 768], P('fsdp')
- grad_value_weight: float32 [768, 768], P('fsdp')
- grad_output_weight: float32 [768, 768], P('fsdp')
- grad_gain_ffn: float32 [768], P('fsdp')
- grad_inner_weight: float32 [768, 3072], P('fsdp')
- grad_outer_weight: float32 [3072, 768], P('fsdp')
Inputs may be any that keep to these rules, and one draw needn't show every extreme that they name: `lengths`: the document of slot s = index % 5 of a pair of blocks has more than half and at most all of its slot's rows, the slots holding 512, 256, 128, 64 and 64 rows.
All inputs are finite; a program needn't handle non-finite values.
Results may differ from a plain program's by a relative error of at most 0.015.
Values may be sent and summed in bfloat16 or wider, within the bound.
No kernel may reach another device: no remote copies, remote signals or barrier semaphores. Data moves between devices by JAX's collectives and lax.ppermute only.
A program may use at most 256 MiB of HBM per device.

v0:
```python
import jax
import jax.numpy as jnp
from jax import lax
from jax.sharding import PartitionSpec as P

H = 12
DK = 64
BUCKETS = 32
BLOCK = 512


norm_eps = 1e-06
bucket_edges = (12, 16, 23, 32, 46, 64, 91)


def rms_scale(values, gain_vec):
    return (
        values * lax.rsqrt(jnp.mean(values * values, axis=-1, keepdims=True) + norm_eps) * gain_vec
    )


def gelu_tanh(values):
    return jax.nn.gelu(values, approximate=True)


def bucket_of(relative):
    distance = jnp.abs(relative)
    passed = sum(((distance >= edge_value).astype(jnp.int32) for edge_value in bucket_edges))
    return jnp.where(relative > 0, BUCKETS // 2, 0) + jnp.where(
        distance < BUCKETS // 4, distance, BUCKETS // 4 + passed
    )


def row_layout(row_count, lengths):
    row_index = jnp.arange(row_count, dtype=jnp.int32)
    block_id = row_index // BLOCK
    within = row_index % BLOCK
    odd_block = block_id % 2
    part_id = (
        (within >= BLOCK // 2).astype(jnp.int32)
        + (within >= 3 * BLOCK // 4).astype(jnp.int32)
        + (within >= 7 * BLOCK // 8).astype(jnp.int32)
    )
    offset = jnp.where(
        part_id == 0,
        0,
        jnp.where(
            part_id == 1, BLOCK // 2, jnp.where(part_id == 2, 3 * BLOCK // 4, 7 * BLOCK // 8)
        ),
    )
    slot_id = jnp.where(odd_block == 1, part_id + 1, 0)
    offset = jnp.where(odd_block == 1, offset, 0)
    document = block_id // 2 * 5 + slot_id
    doc_ids = jnp.arange(lengths.shape[0], dtype=jnp.int32)
    own_length = jnp.sum(
        jnp.where(document[:, None] == doc_ids[None, :], lengths[None, :], 0), axis=1
    )
    return (document, within - offset < own_length)


def distance_select():
    relative = jnp.arange(2 * BLOCK, dtype=jnp.int32) - (BLOCK - 1)
    return (bucket_of(relative)[:, None] == jnp.arange(BUCKETS, dtype=jnp.int32)[None, :]).astype(
        jnp.float32
    )


def skew_rows(per_distance):
    tiled = jnp.tile(per_distance, BLOCK)[: BLOCK * (2 * BLOCK - 1)].reshape(BLOCK, 2 * BLOCK - 1)
    return tiled[:, BLOCK - 1 :]


def unskew_rows(grid_grad):
    padded = jnp.pad(grid_grad, ((0, 0), (BLOCK - 1, 0))).reshape(-1)
    padded = jnp.pad(padded, (0, BLOCK)).reshape(BLOCK, 2 * BLOCK)
    return jnp.sum(padded, axis=0)


def masked_scores(block_query, block_key, pos_bias, block_doc, block_live):
    scores = (
        jnp.einsum("ihd,jhd->hij", block_query, block_key, preferred_element_type=jnp.float32)
        + pos_bias
    )
    allowed = (block_doc[:, None] == block_doc[None, :]) & block_live[None, :]
    return jnp.where(allowed[None], scores, -1e30)


def local(
    hidden,
    gain_attn,
    rel_table,
    query_weight,
    key_weight,
    value_weight,
    output_weight,
    gain_ffn,
    inner_weight,
    outer_weight,
    lengths,
    cotangent,
):
    row_count = hidden.shape[0]
    blocks = row_count // BLOCK
    head_cols = H * DK
    (
        attn_gain,
        table_full,
        query_full,
        key_full,
        value_full,
        output_full,
        ffn_gain,
        inner_full,
        outer_full,
    ) = (
        lax.all_gather(gain_attn, "fsdp", axis=0, tiled=True),
        lax.all_gather(rel_table, "fsdp", axis=0, tiled=True),
        lax.all_gather(query_weight, "fsdp", axis=0, tiled=True),
        lax.all_gather(key_weight, "fsdp", axis=0, tiled=True),
        lax.all_gather(value_weight, "fsdp", axis=0, tiled=True),
        lax.all_gather(output_weight, "fsdp", axis=0, tiled=True),
        lax.all_gather(gain_ffn, "fsdp", axis=0, tiled=True),
        lax.all_gather(inner_weight, "fsdp", axis=0, tiled=True),
        lax.all_gather(outer_weight, "fsdp", axis=0, tiled=True),
    )
    document, in_use = row_layout(row_count, lengths)
    select_table = distance_select()
    per_distance = jnp.dot(
        select_table,
        table_full.astype(jnp.float32).reshape(BUCKETS, H),
        precision=lax.Precision.HIGHEST,
        preferred_element_type=jnp.float32,
    )
    pos_bias = lax.map(skew_rows, per_distance.T)
    hidden_f = hidden.astype(jnp.float32)
    normed, norm_back_a = jax.vjp(rms_scale, hidden_f, attn_gain.astype(jnp.float32))
    normed_low = normed.astype(jnp.bfloat16)
    query = jnp.dot(normed_low, query_full, preferred_element_type=jnp.float32).astype(jnp.bfloat16)
    keyset = jnp.dot(normed_low, key_full, preferred_element_type=jnp.float32).astype(jnp.bfloat16)
    values = jnp.dot(normed_low, value_full, preferred_element_type=jnp.float32).astype(
        jnp.bfloat16
    )
    query_blocks = query.reshape(blocks, BLOCK, H, DK)
    key_blocks = keyset.reshape(blocks, BLOCK, H, DK)
    value_blocks = values.reshape(blocks, BLOCK, H, DK)
    doc_blocks = document.reshape(blocks, BLOCK)
    live_blocks = in_use.reshape(blocks, BLOCK)

    def attend(pieces):
        block_query, block_key, block_value, block_doc, block_live = pieces
        scores = masked_scores(block_query, block_key, pos_bias, block_doc, block_live)
        row_max = jnp.max(scores, axis=-1, keepdims=True)
        expo_terms = jnp.exp(scores - row_max)
        row_total = jnp.sum(expo_terms, axis=-1, keepdims=True)
        attn_probs = (expo_terms / row_total).astype(jnp.bfloat16)
        mixture = jnp.einsum(
            "hij,jhd->ihd", attn_probs, block_value, preferred_element_type=jnp.float32
        )
        return (
            mixture.reshape(BLOCK, head_cols).astype(jnp.bfloat16),
            (row_max + jnp.log(row_total))[..., 0],
        )

    context_blocks, lse_blocks = lax.map(
        attend, (query_blocks, key_blocks, value_blocks, doc_blocks, live_blocks)
    )
    context = context_blocks.reshape(row_count, head_cols)
    middle = hidden_f + jnp.dot(context, output_full, preferred_element_type=jnp.float32)
    normed2, norm_back_f = jax.vjp(rms_scale, middle, ffn_gain.astype(jnp.float32))
    normed2_low = normed2.astype(jnp.bfloat16)
    inner_pre = jnp.dot(normed2_low, inner_full, preferred_element_type=jnp.float32)
    active, gelu_back = jax.vjp(gelu_tanh, inner_pre)
    active_low = active.astype(jnp.bfloat16)
    result = middle + jnp.dot(active_low, outer_full, preferred_element_type=jnp.float32)
    query_full, key_full, value_full, output_full, inner_full, outer_full = (
        lax.all_gather(query_weight, "fsdp", axis=0, tiled=True),
        lax.all_gather(key_weight, "fsdp", axis=0, tiled=True),
        lax.all_gather(value_weight, "fsdp", axis=0, tiled=True),
        lax.all_gather(output_weight, "fsdp", axis=0, tiled=True),
        lax.all_gather(inner_weight, "fsdp", axis=0, tiled=True),
        lax.all_gather(outer_weight, "fsdp", axis=0, tiled=True),
    )
    seed_grad = cotangent.astype(jnp.float32) * in_use[:, None].astype(jnp.float32)
    seed_low = seed_grad.astype(jnp.bfloat16)
    grad_outer = jnp.einsum("tf,td->fd", active_low, seed_low, preferred_element_type=jnp.float32)
    d_active = jnp.einsum("td,fd->tf", seed_low, outer_full, preferred_element_type=jnp.float32)
    d_inner = gelu_back(d_active)[0].astype(jnp.bfloat16)
    grad_inner = jnp.einsum("td,tf->df", normed2_low, d_inner, preferred_element_type=jnp.float32)
    d_normed2 = jnp.einsum("tf,df->td", d_inner, inner_full, preferred_element_type=jnp.float32)
    d_middle_norm, grad_gain_f = norm_back_f(d_normed2)
    d_middle = seed_grad + d_middle_norm
    d_attended = d_middle.astype(jnp.bfloat16)
    grad_output = jnp.einsum("tc,td->cd", context, d_attended, preferred_element_type=jnp.float32)
    d_context = jnp.einsum(
        "td,cd->tc", d_attended, output_full, preferred_element_type=jnp.float32
    ).astype(jnp.bfloat16)

    def attend_back(grid_sum, pieces):
        block_query, block_key, block_value, block_grad, block_doc, block_live, block_lse = pieces
        scores = masked_scores(block_query, block_key, pos_bias, block_doc, block_live)
        attn_probs = jnp.exp(scores - block_lse[:, :, None])
        probs_low = attn_probs.astype(jnp.bfloat16)
        d_probs = jnp.einsum(
            "ihd,jhd->hij", block_grad, block_value, preferred_element_type=jnp.float32
        )
        d_value_blk = jnp.einsum(
            "hij,ihd->jhd", probs_low, block_grad, preferred_element_type=jnp.float32
        )
        center = jnp.sum(attn_probs * d_probs, axis=-1, keepdims=True)
        d_scores = (attn_probs * (d_probs - center)).astype(jnp.bfloat16)
        d_query_blk = jnp.einsum(
            "hij,jhd->ihd", d_scores, block_key, preferred_element_type=jnp.float32
        )
        d_key_blk = jnp.einsum(
            "hij,ihd->jhd", d_scores, block_query, preferred_element_type=jnp.float32
        )
        outputs_blk = (
            d_query_blk.reshape(BLOCK, head_cols).astype(jnp.bfloat16),
            d_key_blk.reshape(BLOCK, head_cols).astype(jnp.bfloat16),
            d_value_blk.reshape(BLOCK, head_cols).astype(jnp.bfloat16),
        )
        return (grid_sum + d_scores.astype(jnp.float32), outputs_blk)

    grid_sum, (d_query, d_key, d_value) = lax.scan(
        attend_back,
        jnp.zeros((H, BLOCK, BLOCK), jnp.float32),
        (
            query_blocks,
            key_blocks,
            value_blocks,
            d_context.reshape(blocks, BLOCK, H, DK),
            doc_blocks,
            live_blocks,
            lse_blocks,
        ),
    )
    d_query = d_query.reshape(row_count, head_cols)
    d_key = d_key.reshape(row_count, head_cols)
    d_value = d_value.reshape(row_count, head_cols)
    dist_grad = lax.map(unskew_rows, grid_sum)
    grad_table = jnp.dot(
        select_table.T,
        dist_grad.T,
        precision=lax.Precision.HIGHEST,
        preferred_element_type=jnp.float32,
    ).reshape(BUCKETS * H)
    grad_query = jnp.einsum("td,tc->dc", normed_low, d_query, preferred_element_type=jnp.float32)
    grad_key = jnp.einsum("td,tc->dc", normed_low, d_key, preferred_element_type=jnp.float32)
    grad_value = jnp.einsum("td,tc->dc", normed_low, d_value, preferred_element_type=jnp.float32)
    d_normed = jnp.einsum("tc,dc->td", d_query, query_full, preferred_element_type=jnp.float32)
    d_normed = d_normed + jnp.einsum(
        "tc,dc->td", d_key, key_full, preferred_element_type=jnp.float32
    )
    d_normed = d_normed + jnp.einsum(
        "tc,dc->td", d_value, value_full, preferred_element_type=jnp.float32
    )
    d_hidden_norm, grad_gain_a = norm_back_a(d_normed)
    grad_hidden = d_middle + d_hidden_norm
    summed = (
        lax.psum(grad_gain_a.astype(jnp.bfloat16), "dp").astype(jnp.float32),
        lax.psum(grad_table.astype(jnp.bfloat16), "dp").astype(jnp.float32),
        lax.psum(grad_query.astype(jnp.bfloat16), "dp").astype(jnp.float32),
        lax.psum(grad_key.astype(jnp.bfloat16), "dp").astype(jnp.float32),
        lax.psum(grad_value.astype(jnp.bfloat16), "dp").astype(jnp.float32),
        lax.psum(grad_output.astype(jnp.bfloat16), "dp").astype(jnp.float32),
        lax.psum(grad_gain_f.astype(jnp.bfloat16), "dp").astype(jnp.float32),
        lax.psum(grad_inner.astype(jnp.bfloat16), "dp").astype(jnp.float32),
        lax.psum(grad_outer.astype(jnp.bfloat16), "dp").astype(jnp.float32),
    )
    shards = (
        lax.psum_scatter(summed[0], "fsdp", scatter_dimension=0, tiled=True),
        lax.psum_scatter(summed[1], "fsdp", scatter_dimension=0, tiled=True),
        lax.psum_scatter(summed[2], "fsdp", scatter_dimension=0, tiled=True),
        lax.psum_scatter(summed[3], "fsdp", scatter_dimension=0, tiled=True),
        lax.psum_scatter(summed[4], "fsdp", scatter_dimension=0, tiled=True),
        lax.psum_scatter(summed[5], "fsdp", scatter_dimension=0, tiled=True),
        lax.psum_scatter(summed[6], "fsdp", scatter_dimension=0, tiled=True),
        lax.psum_scatter(summed[7], "fsdp", scatter_dimension=0, tiled=True),
        lax.psum_scatter(summed[8], "fsdp", scatter_dimension=0, tiled=True),
    )
    return (
        result,
        grad_hidden,
        shards[0],
        shards[1],
        shards[2],
        shards[3],
        shards[4],
        shards[5],
        shards[6],
        shards[7],
        shards[8],
    )


def solution(mesh):
    in_specs = (
        P(("dp", "fsdp"), None),
        P("fsdp"),
        P("fsdp"),
        P("fsdp", None),
        P("fsdp", None),
        P("fsdp", None),
        P("fsdp", None),
        P("fsdp"),
        P("fsdp", None),
        P("fsdp", None),
        P(("dp", "fsdp")),
        P(("dp", "fsdp"), None),
    )
    out_specs = (
        P(("dp", "fsdp"), None),
        P(("dp", "fsdp"), None),
        P("fsdp"),
        P("fsdp"),
        P("fsdp", None),
        P("fsdp", None),
        P("fsdp", None),
        P("fsdp", None),
        P("fsdp"),
        P("fsdp", None),
        P("fsdp", None),
    )
    return jax.shard_map(local, mesh=mesh, in_specs=in_specs, out_specs=out_specs, check_vma=False)
```

profile of v0, /device:TPU:0, one launch (start us, length us, event | category | flops | bytes accessed | tf_op | source)
XLA Modules:
  0.0 1523.9 jit_solution(3161852802505138338)
XLA Ops:
  17.8 44.2 %all-reduce.9 = (bf16[768]{0:T(1024)(128)(2,1)S(1)}, bf16[384]{0:T(512)(128)(2,1)S(1)}, bf16[768]{0:T(1024)(128)(2,1)S(1)}) all-reduce(bf16[768]{0:T(1024)(128)(2,1)S(1)} %dynamic-update-slice, bf16[384]{0:T(512)(128)(2,1)S(1)} %dynamic-update-slice.1, bf16[768]{0:T(1024)(128)(2,1)S(1)} %dynamic-update-slice.2), channel_id=1, replica_groups=mesh['dp'=2,'fsdp'=16] {'fsdp'}, use_global_device_ids=true, to_apply=%add.2 | all-reduce | flops 1920 | bytes 7680
  66.9 78.9 %while.51 = (s32[]{:T(128)}, f32[12,512,512]{1,2,0:T(8,128)}, f32[12,1024]{1,0:T(8,128)S(1)}, s32[]{:T(128)}) while((s32[]{:T(128)}, f32[12,512,512]{1,2,0:T(8,128)}, f32[12,1024]{1,0:T(8,128)S(1)}, s32[]{:T(128)}) %tuple.107), condition=%wide.region_3.4_spmd, body=%wide.region_2.3_spmd.sunk | while | flops 2 | bytes 16785476 | solution.py:134
  167.7 17.7 %all-gather.7.cloned.1.call-done = bf16[768,768]{1,0:T(8,128)(2,1)} async-done(((bf16[48,768]{1,0:T(8,128)(2,1)}), bf16[768,768]{1,0:T(8,128)(2,1)}) %all-gather.7.cloned.1.call-update) | async-done | bytes 1179664 | tf_op jit(solution)/shard_map/all_gather | solution.py:120
  200.5 28.2 %while.52 = (s32[]{:T(128)}, bf16[2,512,768]{2,1,0:T(8,128)(2,1)}, f32[2,12,512]{2,1,0:T(8,128)S(1)}, bf16[2,512,12,64]{1,3,2,0:T(8,128)(2,1)}, s32[2,512]{1,0:T...) while((s32[]{:T(128)}, bf16[2,512,768]{2,1,0:T(8,128)(2,1)}, ...), condition=%wide.region_7.8_spmd, body=%wide.region_4.7_spmd.sunk | while | flops 831383552 | bytes 63685276 | solution.py:164
  228.6 14.5 all-gather.13.cloned.1.call-done
  248.6 76.5 %all-gather.15.cloned.1.call-done = bf16[768,3072]{1,0:T(8,128)(2,1)} async-done(((bf16[48,3072]{1,0:T(8,128)(2,1)}), bf16[768,3072]{1,0:T(8,128)(2,1)}) %all-gather.15.cloned.1.call-update) | async-done | bytes 4718608 | tf_op jit(solution)/shard_map/all_gather | solution.py:123
  338.0 10.2 convolution_convert_fusion.2
  348.3 58.7 %all-gather.17.cloned.1.call-done = bf16[3072,768]{1,0:T(8,128)(2,1)} async-done(((bf16[192,768]{1,0:T(8,128)(2,1)}), bf16[3072,768]{1,0:T(8,128)(2,1)}) %all-gather.17.cloned.1.call-update) | async-done | bytes 4718608 | tf_op jit(solution)/shard_map/all_gather | solution.py:124
  407.0 17.3 %fusion.42 = bf16[1024,3072]{1,0:T(8,128)(2,1)S(1)} fusion(f32[1024,3072]{1,0:T(8,128)} %copy-done.6, bf16[3072,768]{1,0:T(8,128)(2,1)} %all-gather.17.cloned.1.call-done, bf16[1024,768]{0,1:T(8,128)(2,1)} %copy.127, f32[1024]{0:T(1024)S(1)} %copy-done.30), kind=kOutput, calls=%fused_computation.68 | convolution fusion | flops 4897112064 | bytes 25169920 | tf_op jit(solution)/shard_map/td,fd->tf/dot_general | solution.py:186
  433.7 9.9 multiply_reduce_fusion.1
  463.4 106.3 %while.54 = (s32[]{:T(128)}, f32[12,512,512]{1,2,0:T(8,128)}, bf16[2,512,768]{2,1,0:T(8,128)(2,1)}, bf16[2,512,768]{2,1,0:T(8,128)(2,1)}, bf16[2,512,768]{2,1,0:...) while((s32[]{:T(128)}, f32[12,512,512]{1,2,0:T(8,128)}, ...), condition=%wide.region_12.13_spmd.clone, body=%wide.region_10.12_spmd.clone.sunk | while | flops 2052712448 | bytes 181544688 | solution.py:224
  466.9 9.9 multiply_reduce_fusion.5
  484.6 13.6 select_add_fusion.3
  518.0 9.9 multiply_reduce_fusion.5
  535.7 17.6 %select_add_fusion.3 = (f32[12,512,512]{1,2,0:T(8,128)}, bf16[12,512,512]{1,2,0:T(8,128)(2,1)}) fusion(f32[12,512,512]{1,2,0:T(8,128)} %get-tuple-element.716, pred[]{:T(512)S(6)} %compare.33, f32[12,512,512]{1,2,0:T(8,128)} %get-tuple-element.652, f32[12,512,512]{1,2,0:T(8,128)S(1)} %fusion.165, f32[12,512]{1,0:T(8,128)S(1)} %get-tuple-element.653), kind=kLoop, calls=%fused_computation.24.clone.1 | loop fusion | flops 18874368 | bytes 56647680 | tf_op jit(solution)/shard_map/while/body/eval_jaxpr/add | solution.py:222
  579.3 51.8 %all-reduce.14.cloned.1.call-done = (bf16[768,768]{1,0:T(8,128)(2,1)}, bf16[768,768]{1,0:T(8,128)(2,1)}, bf16[768,768]{1,0:T(8,128)(2,1)}, bf16[768,768]{1,0:T(8...) async-done(((bf16[768,768]{1,0:T(8,128)(2,1)}, bf16[768,768]{1,0:T(8,128)(2,1)}, bf16[768,768]{1,0:T(8,128)(2,1)}, bf16[768,768]{1,0:T(8,128)(2,1)}, ...) | async-done | bytes 14155792 | tf_op jit(solution)/shard_map/psum | solution.py:262
  655.2 11.6 convolution_add_fusion
  670.3 117.7 %while.53 = (s32[]{:T(128)}, f32[12,1024]{1,0:T(8,128)S(1)}, f32[12,512,512]{1,2,0:T(8,128)}, s32[]{:T(128)}, f32[]{:T(128)}, /*index=5*/s32[]{:T(128)}) while((s32[]{:T(128)}, f32[12,1024]{1,0:T(8,128)S(1)}, f32[12,512,512]{1,2,0:T(8,128)}, s32[]{:T(128)}, f32[]{:T(128)}, /*index=5*/s32[]{:T(128)}) %tuple.116), condition=%wide.region_19.20_spmd, body=%wide.region_17.19_spmd.sunk | while | flops 523266 | bytes 22024288 | solution.py:240
  801.9 77.5 %all-reduce.8 = (f32[768]{0:T(1024)S(1)}, f32[384]{0:T(512)S(1)}, f32[768]{0:T(1024)S(1)}) all-reduce(bf16[768]{0:T(1024)(128)(2,1)S(1)} %get-tuple-element.447, bf16[384]{0:T(512)(128)(2,1)S(1)} %get-tuple-element.448, bf16[768]{0:T(1024)(128)(2,1)S(1)} %get-tuple-element.449), channel_id=2, replica_groups=mesh['dp'=2,'fsdp'=16] {'fsdp'}, use_global_device_ids=true, to_apply=%region_16.17.clone | all-reduce | flops 1920 | bytes 11520
  881.2 17.4 %reduce-scatter.9.cloned.1.call-done = f32[48,768]{1,0:T(8,128)} async-done(((f32[768,768]{1,0:T(8,128)}), f32[48,768]{1,0:T(8,128)}) %reduce-scatter.9.cloned.1.call-update) | async-done | bytes 147472 | tf_op jit(solution)/shard_map/reduce_scatter | solution.py:274
  898.6 131.9 %reduce-scatter.11.cloned.1.call-done = f32[48,768]{1,0:T(8,128)} async-done(((f32[768,768]{1,0:T(8,128)}), f32[48,768]{1,0:T(8,128)}) %reduce-scatter.11.cloned.1.call-update) | async-done | bytes 147472 | tf_op jit(solution)/shard_map/reduce_scatter | solution.py:275
  1030.6 132.9 %reduce-scatter.13.cloned.1.call-done = f32[48,768]{1,0:T(8,128)} async-done(((f32[768,768]{1,0:T(8,128)}), f32[48,768]{1,0:T(8,128)}) %reduce-scatter.13.cloned.1.call-update) | async-done | bytes 147472 | tf_op jit(solution)/shard_map/reduce_scatter | solution.py:276
  1163.5 176.3 %reduce-scatter.15.cloned.1.call-done = f32[48,3072]{1,0:T(8,128)} async-done(((f32[768,3072]{1,0:T(8,128)}), f32[48,3072]{1,0:T(8,128)}) %reduce-scatter.15.cloned.1.call-update) | async-done | bytes 589840 | tf_op jit(solution)/shard_map/reduce_scatter | solution.py:278
  1339.8 177.2 %reduce-scatter.17.cloned.1.call-done = f32[192,768]{1,0:T(8,128)} async-done(((f32[3072,768]{1,0:T(8,128)}), f32[192,768]{1,0:T(8,128)}) %reduce-scatter.17.cloned.1.call-update) | async-done | bytes 589840 | tf_op jit(solution)/shard_map/reduce_scatter | solution.py:279
  (409 shorter events, 427.9 us)
Async XLA Ops:
  7.2 57.7 %copy-start.14 = (bf16[1024,768]{1,0:T(8,128)(2,1)S(1)}, bf16[1024,768]{1,0:T(8,128)(2,1)}, u32[]{:S(2)}) copy-start(bf16[1024,768]{1,0:T(8,128)(2,1)} %param.31) | copy-start | bytes 4718596
  7.2 138.6 %all-gather.9.cloned.1.call-start = ((), (), s32[]{:S(2)}) async-start(), calls=%async_computation.7 | async-start | bytes 1253376 | tf_op jit(solution)/shard_map/all_gather | solution.py:118
  7.9 146.1 %all-gather.11.cloned.1.call-start = ((), (), s32[]{:S(2)}) async-start(), calls=%async_computation.8 | async-start | bytes 1253376 | tf_op jit(solution)/shard_map/all_gather | solution.py:119
  8.7 176.8 %all-gather.7.cloned.1.call-start = ((), (), s32[]{:S(2)}) async-start(), calls=%async_computation.6 | async-start | bytes 1253376 | tf_op jit(solution)/shard_map/all_gather | solution.py:120
  9.4 233.8 %all-gather.13.cloned.1.call-start = ((), (), s32[]{:S(2)}) async-start(), calls=%async_computation.9 | async-start | bytes 1253376 | tf_op jit(solution)/shard_map/all_gather | solution.py:121
  10.0 315.2 %all-gather.15.cloned.1.call-start = ((), (), s32[]{:S(2)}) async-start(), calls=%async_computation.10 | async-start | bytes 5013504 | tf_op jit(solution)/shard_map/all_gather | solution.py:123
  10.6 396.4 %all-gather.17.cloned.1.call-start = ((), (), s32[]{:S(2)}) async-start(), calls=%async_computation.11 | async-start | bytes 5013504 | tf_op jit(solution)/shard_map/all_gather | solution.py:124
  11.1 620.0 %all-reduce.14.cloned.1.call-start = ((), (), s32[]{:S(2)}) async-start(), calls=%async_computation.18 | async-start | bytes 28311552 | tf_op jit(solution)/shard_map/psum | solution.py:262
  11.3 55.3 %copy-start.31 = (s32[1024]{0:T(1024)}, s32[1024]{0:T(1024)S(1)}, u32[]{:S(2)}) copy-start(s32[1024]{0:T(1024)S(1)} %fusion.82) | copy-start | bytes 12292
  62.0 123.4 %copy-start.26 = (f32[768]{0:T(1024)}, f32[768]{0:T(1024)S(1)}, u32[]{:S(2)}) copy-start(f32[768]{0:T(1024)S(1)} %convert_element_type.315) | copy-start | bytes 9220
  64.9 120.5 %copy-start.24 = (f32[1024]{0:T(1024)}, f32[1024]{0:T(1024)S(1)}, u32[]{:S(2)}) copy-start(f32[1024]{0:T(1024)S(1)} %fusion.99) | copy-start | bytes 12292
  243.2 82.0 %copy-start.23 = (f32[768]{0:T(1024)S(1)}, f32[768]{0:T(1024)}, u32[]{:S(2)}) copy-start(f32[768]{0:T(1024)} %convert_element_type.333) | copy-start | bytes 9220
  325.2 12.8 copy-start.12
  325.2 12.8 copy-start.30
  407.0 19.9 %copy-start.7 = (f32[1024,768]{0,1:T(8,128)S(1)}, f32[1024,768]{0,1:T(8,128)}, u32[]{:S(2)}) copy-start(f32[1024,768]{0,1:T(8,128)} %get-tuple-element.467) | copy-start | bytes 9437188
  463.4 106.3 %copy-start.25 = (f32[1024]{0:T(1024)S(1)}, f32[1024]{0:T(1024)}, u32[]{:S(2)}) copy-start(f32[1024]{0:T(1024)} %copy-done.24) | copy-start | bytes 12292
  463.4 106.3 %copy-start.27 = (f32[768]{0:T(1024)S(1)}, f32[768]{0:T(1024)}, u32[]{:S(2)}) copy-start(f32[768]{0:T(1024)} %copy-done.26) | copy-start | bytes 9220
  579.3 301.9 %reduce-scatter.7.cloned.1.call-start = ((), (), s32[]{:S(2)}) async-start(), calls=%async_computation.12 | async-start | bytes 2506752 | tf_op jit(solution)/shard_map/reduce_scatter | solution.py:273
  634.1 264.6 %reduce-scatter.9.cloned.1.call-start = ((), (), s32[]{:S(2)}) async-start(), calls=%async_computation.13 | async-start | bytes 2506752 | tf_op jit(solution)/shard_map/reduce_scatter | solution.py:274
  635.8 394.8 %reduce-scatter.11.cloned.1.call-start = ((), (), s32[]{:S(2)}) async-start(), calls=%async_computation.14 | async-start | bytes 2506752 | tf_op jit(solution)/shard_map/reduce_scatter | solution.py:275
  637.5 526.0 %reduce-scatter.13.cloned.1.call-start = ((), (), s32[]{:S(2)}) async-start(), calls=%async_computation.15 | async-start | bytes 2506752 | tf_op jit(solution)/shard_map/reduce_scatter | solution.py:276
  639.1 700.6 %reduce-scatter.15.cloned.1.call-start = ((), (), s32[]{:S(2)}) async-start(), calls=%async_computation.16 | async-start | bytes 10027008 | tf_op jit(solution)/shard_map/reduce_scatter | solution.py:278
  646.5 870.5 %reduce-scatter.17.cloned.1.call-start = ((), (), s32[]{:S(2)}) async-start(), calls=%async_computation.17 | async-start | bytes 10027008 | tf_op jit(solution)/shard_map/reduce_scatter | solution.py:279
  670.3 117.7 %copy-start.32 = (s32[1024]{0:T(1024)S(1)}, s32[1024]{0:T(1024)}, u32[]{:S(2)}) copy-start(s32[1024]{0:T(1024)} %copy-done.31) | copy-start | bytes 12292
  (29 other events, 93.6 us)
Sparse Core Ops, SparseCore 0:
  10.8 58.9 all-gather.8
  72.6 54.9 all-gather.10
  130.4 54.9 all-gather.6
  188.1 54.9 all-gather.12
  245.8 79.3 all-gather.14
  327.8 79.0 all-gather.16
  579.4 51.7 all-reduce.13
  636.6 128.9 reduce-scatter.6
  771.8 126.7 reduce-scatter.8
  904.0 126.5 reduce-scatter.10
  1036.8 126.5 reduce-scatter.12
  1169.6 170.1 reduce-scatter.14
  1347.0 169.9 reduce-scatter.16
where the time goes:
time: 1540 us; the launch traced here: 1520 us
  waiting for transfers between devices  859 us (56%)
  local copies, waits for them, and re-layouts  279 us (18%)
  matrix products  178 us (12%)
  blocking collectives  124 us (8%)
  other arithmetic  63.4 us (4%)
  between operations  17.7 us (1%)
    reduce_scatter x1, waiting for transfers between devices, local(): lax.psum_scatter(summed[8], 'fsdp', scatter_dimension=0, tiled=True)  177 us
    reduce_scatter x1, waiting for transfers between devices, local(): lax.psum_scatter(summed[7], 'fsdp', scatter_dimension=0, tiled=True)  176 us
    reduce_scatter x1, waiting for transfers between devices, local(): lax.psum_scatter(summed[5], 'fsdp', scatter_dimension=0, tiled=True)  133 us
    reduce_scatter x1, waiting for transfers between devices, local(): lax.psum_scatter(summed[4], 'fsdp', scatter_dimension=0, tiled=True)  132 us
    unnamed x2, blocking collectives  122 us
    all_gather x1, waiting for transfers between devices, local(): lax.all_gather(inner_weight, 'fsdp', axis=0, tiled=True)  76.5 us
    all_gather x1, waiting for transfers between devices, local(): lax.all_gather(outer_weight, 'fsdp', axis=0, tiled=True)  58.7 us
    psum x1, waiting for transfers between devices, local(): lax.psum(grad_query.astype(jnp.bfloat16), 'dp').astype(jnp.float32)  51.8 us
  transfers between devices with their start and end apart: 13, of which 10 were waited for; matrix products, arithmetic and copies ran while one was open for 22% of the time, Pallas kernels for 0%

commit v1 on v0

v1 whole, which is shorter than its diff:
```python
import functools

import jax
import jax.numpy as jnp
import numpy as np
from jax import lax
from jax.experimental import pallas as pl
from jax.experimental.pallas import tpu as pltpu
from jax.sharding import PartitionSpec as P

H = 12
DK = 64
BUCKETS = 32
BLOCK = 512
norm_eps = 1e-06
bucket_edges = (12, 16, 23, 32, 46, 64, 91)
MASKED = -1e30
F32 = jnp.float32
BF16 = jnp.bfloat16
PAIR = 2 * BLOCK
GROUPS = ((0, 512), (512, 256), (768, 128), (896, 128))
SPAN = 1024
VMEM_BIG = 58 * 1024 * 1024


def bucket_of(relative):
    distance = jnp.abs(relative)
    passed = sum(((distance >= edge_value).astype(jnp.int32) for edge_value in bucket_edges))
    return jnp.where(relative > 0, BUCKETS // 2, 0) + jnp.where(
        distance < BUCKETS // 4, distance, BUCKETS // 4 + passed
    )


class Ring:
    def __init__(self, mesh):
        self.cores = mesh.shape["dp"]
        self.n = mesh.shape["fsdp"]
        bits = self.n.bit_length() - 1
        base = list(range(bits - 1, -1, -1))
        other = base[:-2] + base[-2:][::-1]
        self.order = (base, other)
        self.bits = bits

    def offsets(self, which):
        out = np.zeros(self.n, np.int32)
        for j in range(self.n):
            for k, b in enumerate(self.order[which]):
                out[j] |= ((j >> k) & 1) << b
        return out

    def inverse(self, which):
        off = self.offsets(which)
        inv = np.zeros(self.n, np.int32)
        inv[off] = np.arange(self.n)
        return inv

    def swap_phase(self, k):
        n = self.n
        return [
            (c * n + f, c * n + (f ^ (1 << self.order[c][k])))
            for c in range(2)
            for f in range(n)
        ]

    def swap_core(self):
        n = self.n
        return [(c * n + f, (1 - c) * n + f) for c in range(2) for f in range(n)]

    def meta(self):
        me = lax.axis_index("fsdp").astype(jnp.int32)
        core = lax.axis_index("dp").astype(jnp.int32)
        spots = jnp.arange(self.n, dtype=jnp.int32)

        def off(which):
            out = jnp.zeros_like(spots)
            for k, b in enumerate(self.order[which]):
                out = out | (((spots >> k) & 1) << b)
            return out

        def inv(which, m):
            out = jnp.zeros_like(spots)
            for k, b in enumerate(self.order[which]):
                out = out | (((m >> b) & 1) << k)
            return out

        first = core == 0
        mixed = me ^ spots
        return jnp.concatenate(
            [
                core[None],
                me ^ jnp.where(first, off(0), off(1)),
                me ^ jnp.where(first, off(1), off(0)),
                jnp.where(first, inv(0, mixed), inv(1, mixed)),
                jnp.where(first, inv(1, mixed), inv(0, mixed)),
            ]
        )


    def flip_origin(self, pieces):
        me = lax.axis_index("fsdp")
        shape = pieces.shape
        pieces = pieces.reshape((2,) * self.bits + shape[1:])
        for b in range(self.bits):
            axis = self.bits - 1 - b
            pieces = jnp.where((me >> b) & 1 == 1, jnp.flip(pieces, axis), pieces)
        return pieces.reshape(shape)

    def reorder(self, pieces, first, back):
        shape = pieces.shape
        split = pieces.reshape((2,) * self.bits + shape[1:])
        tail = list(range(self.bits, self.bits + len(shape) - 1))
        found = []
        for order in self.order:
            axes = [self.bits - 1 - order.index(self.bits - 1 - a) for a in range(self.bits)]
            if back:
                axes = list(np.argsort(axes))
            found.append(jnp.transpose(split, [int(a) for a in axes] + tail).reshape(shape))
        return jnp.where(first, found[0], found[1])

    def to_origin(self, pieces, first):
        return self.flip_origin(self.reorder(pieces, first, False))

    def from_origin(self, pieces, first):
        return self.reorder(self.flip_origin(pieces), first, True)


def shift(value, pairs):
    return lax.ppermute(value, ("dp", "fsdp"), pairs)


def gather_pieces(ring, shard):
    held = shard[None]
    for k in range(ring.bits - 1):
        held = jnp.concatenate([held, shift(held, ring.swap_phase(k))], axis=0)
    last = shift(held, ring.swap_phase(ring.bits - 1))
    return (held, last), (shift(held, ring.swap_core()), shift(last, ring.swap_core()))


def reduce_pieces(ring, keep, send):
    got = shift(send, ring.swap_core())
    count = ring.n
    for k in range(ring.bits - 1, -1, -1):
        half = count // 2
        away = (keep[half:count].astype(F32) + got[half:count].astype(F32)).astype(BF16)
        stay = (keep[:half].astype(F32) + got[:half].astype(F32)).astype(BF16)
        if k == 0:
            stay = keep[:half].astype(F32) + got[:half].astype(F32)
        got = shift(away, ring.swap_phase(k))
        keep = stay
        count = half
    return keep[0].astype(F32) + got[0].astype(F32)


def any_spec():
    return pl.BlockSpec(memory_space=pl.ANY)


def params(vmem=VMEM_BIG):
    return pltpu.CompilerParams(vmem_limit_bytes=vmem)


def cost(flops, bytes_accessed, trans=0):
    return pl.CostEstimate(flops=flops, bytes_accessed=bytes_accessed, transcendentals=trans)


def dot(a, b):
    return jnp.dot(a, b, preferred_element_type=F32)


def dot_nt(a, b):
    return lax.dot_general(a, b, (((1,), (1,)), ((), ())), preferred_element_type=F32)


def dot_tn(a, b):
    return lax.dot_general(a, b, (((0,), (0,)), ((), ())), preferred_element_type=F32)


class Pieces:
    def __init__(self, own, rec, n):
        self.arrays = [own[0], own[1], rec[0], rec[1]]
        self.n = n
        self.count = 4
        self.whole = False


class Whole:
    def __init__(self, array):
        self.arrays = [array]
        self.count = 1
        self.whole = True
        self.n = 0


def column_copies(chunk, meta, refs, lo, width, dst, sems, base=0):
    copies = []
    if chunk.whole:
        for h in range(2):
            src = refs[0].at[h, :, pl.ds(lo, width)]
            copies.append(
                pltpu.make_async_copy(src, dst.at[:, pl.ds(h * width, width)], sems.at[base + h])
            )
        return copies
    n = chunk.n
    half = n // 2
    rows = refs[0].shape[1]
    core = meta[0]
    for h in range(2):
        col = pl.multiple_of((core if h == 0 else 1 - core) * width, 128)
        for j in range(n):
            ref = refs[2 * h + j // half]
            row = pl.multiple_of(meta[1 + h * n + j] * rows, 16)
            copies.append(
                pltpu.make_async_copy(
                    ref.at[j % half, :, pl.ds(lo, width)],
                    dst.at[pl.ds(row, rows), pl.ds(col, width)],
                    sems.at[base + h * n + j],
                )
            )
    return copies


def row_copies(chunk, meta, refs, dst, sems, base=0):
    if chunk.whole:
        return [pltpu.make_async_copy(refs[0], dst, sems.at[base])]
    n = chunk.n
    half = n // 2
    rows = refs[0].shape[1]
    core = meta[0]
    copies = []
    for h in range(2):
        for j in range(n):
            ref = refs[2 * h + j // half]
            row = pl.multiple_of(
                meta[1 + h * n + j] * (2 * rows) + (core if h == 0 else 1 - core) * rows, 16
            )
            copies.append(
                pltpu.make_async_copy(
                    ref.at[j % half], dst.at[pl.ds(row, rows), :], sems.at[base + h * n + j]
                )
            )
    return copies


def run_copies(copies):
    for c in copies:
        c.start()
    for c in copies:
        c.wait()


def copy_count(chunk):
    return 2 if chunk.whole else 2 * chunk.n


def norm_tile(x, ext_ref, first):
    d = x.shape[1]
    scale = lax.rsqrt(jnp.mean(x * x, axis=-1, keepdims=True) + norm_eps)
    out = []
    for c in range(d // 128):
        out.append(
            (x[:, c * 128 : (c + 1) * 128] * scale * ext_ref[first + c : first + c + 1, :]).astype(
                BF16
            )
        )
    return jnp.concatenate(out, axis=1), scale


def qkv_kernel(chunk, meta, x_ref, ext_ref, *rest):
    refs = rest[: chunk.count]
    qkv_ref, n_ref, dist_ref, w, sems = rest[chunk.count :]
    width = w.shape[1] // 2

    @pl.when(pl.program_id(0) == 0)
    def _():
        copies = column_copies(chunk, meta, refs, 0, width, w, sems)
        for c in copies:
            c.start()
        place = lax.broadcasted_iota(jnp.int32, (BUCKETS, SPAN), 1)
        row = lax.broadcasted_iota(jnp.int32, (BUCKETS, SPAN), 0)
        chosen = (bucket_of(BLOCK - 1 - place) == row).astype(F32).astype(BF16)
        dist_ref[...] = dot(ext_ref[16:32, 0:BUCKETS].astype(BF16), chosen)
        for c in copies:
            c.wait()

    normed, _ = norm_tile(x_ref[...].astype(F32), ext_ref, 0)
    n_ref[...] = normed
    qkv_ref[...] = dot(normed, w[...]).astype(BF16)


def qkv_call(meta, x, ext, chunk, tile=256):
    rows, d = x.shape
    grid_spec = pltpu.PrefetchScalarGridSpec(
        num_scalar_prefetch=1,
        grid=(rows // tile,),
        in_specs=[
            pl.BlockSpec((tile, d), lambda i, m: (i, 0)),
            pl.BlockSpec(ext.shape, lambda i, m: (0, 0)),
        ]
        + [any_spec()] * chunk.count,
        out_specs=[
            pl.BlockSpec((tile, 3 * d), lambda i, m: (i, 0)),
            pl.BlockSpec((tile, d), lambda i, m: (i, 0)),
            pl.BlockSpec((16, SPAN), lambda i, m: (0, 0)),
        ],
        scratch_shapes=[
            pltpu.VMEM((d, 3 * d), BF16),
            pltpu.SemaphoreType.DMA((copy_count(chunk),)),
        ],
    )
    return pl.pallas_call(
        functools.partial(qkv_kernel, chunk),
        grid_spec=grid_spec,
        out_shape=[
            jax.ShapeDtypeStruct((rows, 3 * d), BF16),
            jax.ShapeDtypeStruct((rows, d), BF16),
            jax.ShapeDtypeStruct((16, SPAN), F32),
        ],
        compiler_params=params(),
        cost_estimate=cost(6 * rows * d * d, 14 * rows * d + 6 * d * d),
        name="qkv",
    )(meta, x, ext, *chunk.arrays)


def bias_strip(dist_row):
    spread = jnp.broadcast_to(dist_row, (128, SPAN))
    return pltpu.roll(spread, SPAN - 127, 1, stride=1, stride_axis=0)


def attend_kernel(q_ref, k_ref, v_ref, qaug_ref, kaug_ref, dist_ref, ctx_ref, lse_ref):
    pair = pl.program_id(1)
    lane = lax.broadcasted_iota(jnp.int32, (PAIR, 128), 1)
    q, k = q_ref[...], k_ref[...]
    qaug, kaug = qaug_ref[...], kaug_ref[...]
    v_turned = v_ref[...].T
    heads = []
    for hh in range(2):
        mine = (lane // 64) == hh
        heads.append(
            (
                jnp.where(mine, q, qaug),
                jnp.where(mine, k, kaug),
                v_turned[hh * 64 : (hh + 1) * 64, :],
                bias_strip(dist_ref[pl.ds(2 * pair + hh, 1), :]),
            )
        )
    for off, size in GROUPS:
        step = min(256, size)
        for i0 in range(0, size, step):
            parts = []
            for hh in range(2):
                qa, ka, vt, strip = heads[hh]
                scores = dot_nt(ka[off : off + size], qa[off + i0 : off + i0 + step])
                bias = jnp.concatenate(
                    [
                        strip[:, (3 - t) * 128 + i0 : (3 - t) * 128 + i0 + step]
                        for t in range(size // 128)
                    ],
                    axis=0,
                )
                scores = scores + bias
                top = jnp.max(scores, axis=0, keepdims=True)
                expo = jnp.exp(scores - top)
                total = jnp.sum(expo, axis=0, keepdims=True)
                mixed = dot(vt[:, off : off + size], expo.astype(BF16))
                parts.append(mixed * (1.0 / total))
                lse_ref[0, hh : hh + 1, off + i0 : off + i0 + step] = top + jnp.log(total)
            both = jnp.concatenate(parts, axis=0)
            ctx_ref[off + i0 : off + i0 + step, :] = both.T.astype(BF16)


def head_block(part):
    return lambda p, h: (p, (h // 3) * 9 + part * 3 + h % 3)


def attend_call(qkv, qaug, kaug, dist):
    rows = qkv.shape[0]
    d = qkv.shape[1] // 3
    pairs = rows // PAIR
    return pl.pallas_call(
        attend_kernel,
        grid=(pairs, H // 2),
        in_specs=[
            pl.BlockSpec((PAIR, 128), head_block(0)),
            pl.BlockSpec((PAIR, 128), head_block(1)),
            pl.BlockSpec((PAIR, 128), head_block(2)),
            pl.BlockSpec((PAIR, 128), lambda p, h: (p, 0)),
            pl.BlockSpec((PAIR, 128), lambda p, h: (p, 0)),
            pl.BlockSpec((16, SPAN), lambda p, h: (0, 0)),
        ],
        out_specs=[
            pl.BlockSpec((PAIR, 128), lambda p, h: (p, h)),
            pl.BlockSpec((1, 2, PAIR), lambda p, h: (h, 0, p)),
        ],
        out_shape=[
            jax.ShapeDtypeStruct((rows, d), BF16),
            jax.ShapeDtypeStruct((H // 2, 2, rows), F32),
        ],
        compiler_params=params(),
        cost_estimate=cost(4 * pairs * H * 350000 * 128, 8 * rows * d, pairs * H * 350000),
        name="attend",
    )(qkv, qkv, qkv, qaug, kaug, dist)


def mid_kernel(chunk, meta, ctx_ref, x_ref, ext_ref, *rest):
    refs = rest[: chunk.count]
    mid_ref, n2_ref, act_ref, slope_ref, wo, w1, sems = rest[chunk.count :]
    d = wo.shape[0]

    @pl.when(pl.program_id(0) == 0)
    def _():
        n = copy_count(chunk)
        run_copies(
            column_copies(chunk, meta, refs, 0, d // 2, wo, sems)
            + column_copies(chunk, meta, refs, d // 2, w1.shape[1] // 2, w1, sems, n)
        )

    middle = x_ref[...].astype(F32) + dot(ctx_ref[...], wo[...])
    mid_ref[...] = middle
    normed, _ = norm_tile(middle, ext_ref, 6)
    n2_ref[...] = normed
    c0 = 0.7978845608028654
    c1 = c0 * 0.044715
    step = 512
    for f in range(0, w1.shape[1], step):
        v = dot(normed, w1[:, f : f + step])
        v2 = v * v
        t = jnp.tanh(v * (c0 + c1 * v2))
        half = 0.5 + 0.5 * t
        act_ref[:, f : f + step] = (v * half).astype(BF16)
        slope_ref[:, f : f + step] = (
            half + (0.5 * v) * (1.0 - t * t) * (c0 + (3.0 * c1) * v2)
        ).astype(BF16)


def mid_call(meta, ctx, x, ext, chunk, ff, tile=256):
    rows, d = x.shape
    grid_spec = pltpu.PrefetchScalarGridSpec(
        num_scalar_prefetch=1,
        grid=(rows // tile,),
        in_specs=[
            pl.BlockSpec((tile, d), lambda i, m: (i, 0)),
            pl.BlockSpec((tile, d), lambda i, m: (i, 0)),
            pl.BlockSpec(ext.shape, lambda i, m: (0, 0)),
        ]
        + [any_spec()] * chunk.count,
        out_specs=[
            pl.BlockSpec((tile, d), lambda i, m: (i, 0)),
            pl.BlockSpec((tile, d), lambda i, m: (i, 0)),
            pl.BlockSpec((tile, ff), lambda i, m: (i, 0)),
            pl.BlockSpec((tile, ff), lambda i, m: (i, 0)),
        ],
        scratch_shapes=[
            pltpu.VMEM((d, d), BF16),
            pltpu.VMEM((d, ff), BF16),
            pltpu.SemaphoreType.DMA((2 * copy_count(chunk),)),
        ],
    )
    return pl.pallas_call(
        functools.partial(mid_kernel, chunk),
        grid_spec=grid_spec,
        out_shape=[
            jax.ShapeDtypeStruct((rows, d), F32),
            jax.ShapeDtypeStruct((rows, d), BF16),
            jax.ShapeDtypeStruct((rows, ff), BF16),
            jax.ShapeDtypeStruct((rows, ff), BF16),
        ],
        compiler_params=params(),
        cost_estimate=cost(2 * rows * d * (d + ff), 10 * rows * d + 4 * rows * ff, rows * ff),
        name="mid",
    )(meta, ctx, x, ext, *chunk.arrays)


def outer_grad_kernel(n, meta, act_ref, g_ref, keep_ref, send_ref):
    per = keep_ref.shape[1]
    first = meta[0] == 0
    total = dot_tn(act_ref[...], g_ref[...]).astype(BF16)
    count = act_ref.shape[1] // (2 * per)
    for f in range(count):
        low = total[2 * f * per : (2 * f + 1) * per]
        high = total[(2 * f + 1) * per : (2 * f + 2) * per]
        spot = pl.program_id(0) * count + f
        keep_ref[meta[1 + 2 * n + spot]] = jnp.where(first, low, high)
        send_ref[meta[1 + 3 * n + spot]] = jnp.where(first, high, low)


def outer_grad_call(meta, act, g, n):
    rows, ff = act.shape
    d = g.shape[1]
    per = ff // n // 2
    shape = jax.ShapeDtypeStruct((n, per, d), BF16)
    return pl.pallas_call(
        functools.partial(outer_grad_kernel, n),
        grid_spec=pltpu.PrefetchScalarGridSpec(
            num_scalar_prefetch=1,
            grid=(ff // 768,),
            in_specs=[
                pl.BlockSpec((rows, 768), lambda i, m: (0, i)),
                pl.BlockSpec((rows, d), lambda i, m: (0, 0)),
            ],
            out_specs=[pl.BlockSpec((n, per, d), lambda i, m: (0, 0, 0))] * 2,
        ),
        out_shape=[shape, shape],
        compiler_params=params(),
        cost_estimate=cost(2 * rows * d * ff, 2 * rows * (d + ff) + 2 * d * ff),
        name="outer_grad",
    )(meta, act, g)


def out_kernel(chunk, meta, act_ref, mid_ref, g_ref, slope_ref, *rest):
    refs = rest[: chunk.count]
    result_ref, din_ref, w2, sems = rest[chunk.count :]

    @pl.when(pl.program_id(0) == 0)
    def _():
        run_copies(row_copies(chunk, meta, refs, w2, sems))

    result_ref[...] = mid_ref[...] + dot(act_ref[...], w2[...])
    step = 512
    g = g_ref[...]
    for f in range(0, w2.shape[0], step):
        d_act = dot_nt(g, w2[f : f + step, :])
        din_ref[:, f : f + step] = (d_act * slope_ref[:, f : f + step].astype(F32)).astype(BF16)


def out_call(meta, act, middle, g, slope, chunk, tile=256):
    rows, ff = act.shape
    d = middle.shape[1]
    row = lambda w: pl.BlockSpec((tile, w), lambda i, m: (i, 0))
    return pl.pallas_call(
        functools.partial(out_kernel, chunk),
        grid_spec=pltpu.PrefetchScalarGridSpec(
            num_scalar_prefetch=1,
            grid=(rows // tile,),
            in_specs=[row(ff), row(d), row(d), row(ff)] + [any_spec()] * chunk.count,
            out_specs=[row(d), row(ff)],
            scratch_shapes=[
                pltpu.VMEM((ff, d), BF16),
                pltpu.SemaphoreType.DMA((copy_count(chunk),)),
            ],
        ),
        out_shape=[
            jax.ShapeDtypeStruct((rows, d), F32),
            jax.ShapeDtypeStruct((rows, ff), BF16),
        ],
        compiler_params=params(),
        cost_estimate=cost(4 * rows * d * ff, 10 * rows * d + 6 * rows * ff),
        name="out",
    )(meta, act, middle, g, slope, *chunk.arrays)


def column_grad_kernel(n, steps, extra, meta, a_ref, *rest):
    b_refs = rest[: len(rest) - 3 - (1 if extra else 0)]
    rest = rest[len(b_refs) :]
    e_ref = rest[0] if extra else None
    keep_ref, send_ref, turned = rest[1:] if extra else rest
    half = pl.program_id(0)

    @pl.when((half == 0) & (pl.program_id(1) == 0))
    def _():
        turned[...] = a_ref[...].T

    per = turned.shape[0] // n

    def fill(out, table):
        col = 0
        for b_ref in b_refs:
            w = b_ref.shape[1]
            total = dot(turned[...], b_ref[...]).astype(BF16)
            for f in range(n):
                out[meta[1 + table * n + f], :, col : col + w] = total[f * per : (f + 1) * per]
            col += w
        if extra:
            for f in range(n):
                out[f, :, col : col + 128] = e_ref[...]

    @pl.when(half == 0)
    def _():
        fill(send_ref, 3)

    @pl.when(half == 1)
    def _():
        fill(keep_ref, 2)


def column_grad_call(meta, a, bs, n, steps, name, extra=None):
    rows, d = a.shape
    per = d // n
    widths = [b.shape[1] // 2 // steps for b in bs]
    block = sum(widths) + (128 if extra is not None else 0)
    shape = jax.ShapeDtypeStruct((n, per, block * steps), BF16)

    def pick(i, j, m):
        half = jnp.where(i == 0, 1 - m[0], m[0])
        return (0, half * steps + j)

    in_specs = [pl.BlockSpec((rows, d), lambda i, j, m: (0, 0))]
    in_specs += [pl.BlockSpec((rows, w), pick) for w in widths]
    args = [a, *bs]
    if extra is not None:
        assert steps == 1
        in_specs.append(pl.BlockSpec(extra.shape, lambda i, j, m: (0, 0)))
        args.append(extra)
    return pl.pallas_call(
        functools.partial(column_grad_kernel, n, steps, extra is not None),
        grid_spec=pltpu.PrefetchScalarGridSpec(
            num_scalar_prefetch=1,
            grid=(2, steps),
            in_specs=in_specs,
            out_specs=[
                pl.BlockSpec((n, per, block), lambda i, j, m: (0, 0, jnp.where(i == 0, 0, j))),
                pl.BlockSpec(
                    (n, per, block), lambda i, j, m: (0, 0, jnp.where(i == 0, j, steps - 1))
                ),
            ],
            scratch_shapes=[pltpu.VMEM((d, rows), BF16)],
        ),
        out_shape=[shape, shape],
        compiler_params=params(),
        cost_estimate=cost(
            2 * rows * d * sum(b.shape[1] for b in bs),
            2 * rows * (d + sum(b.shape[1] for b in bs)) + 2 * d * sum(b.shape[1] for b in bs),
        ),
        name=name,
    )(meta, *args)


def norm_back(dn, x, gain_ref, first, scale):
    d = x.shape[1]
    z = jnp.concatenate(
        [
            dn[:, c * 128 : (c + 1) * 128] * gain_ref[first + c : first + c + 1, :]
            for c in range(d // 128)
        ],
        axis=1,
    )
    inner = jnp.mean(z * x, axis=-1, keepdims=True)
    back = scale * z - x * (scale * scale * scale * inner)
    return back, jnp.sum(dn * (x * scale), axis=0, keepdims=True)


def mid_back_kernel(chunk, meta, din_ref, mid_ref, g_ref, ext_ref, *rest):
    refs = rest[: chunk.count]
    dmid_ref, datt_ref, dctx_ref, gain_ref, wo, w1, sems = rest[chunk.count :]
    d = wo.shape[0]

    @pl.when(pl.program_id(0) == 0)
    def _():
        n = copy_count(chunk)
        run_copies(
            column_copies(chunk, meta, refs, 0, d // 2, wo, sems)
            + column_copies(chunk, meta, refs, d // 2, w1.shape[1] // 2, w1, sems, n)
        )
        gain_ref[...] = jnp.zeros_like(gain_ref)

    dn = dot_nt(din_ref[...], w1[...])
    middle = mid_ref[...]
    scale = lax.rsqrt(jnp.mean(middle * middle, axis=-1, keepdims=True) + norm_eps)
    back, gain = norm_back(dn, middle, ext_ref, 6, scale)
    gain_ref[...] += gain
    dmid = g_ref[...].astype(F32) + back
    dmid_ref[...] = dmid
    low = dmid.astype(BF16)
    datt_ref[...] = low
    dctx_ref[...] = dot_nt(low, wo[...]).astype(BF16)


def mid_back_call(meta, din, middle, g, ext, chunk, tile=256):
    rows, ff = din.shape
    d = middle.shape[1]
    row = lambda w: pl.BlockSpec((tile, w), lambda i, m: (i, 0))
    return pl.pallas_call(
        functools.partial(mid_back_kernel, chunk),
        grid_spec=pltpu.PrefetchScalarGridSpec(
            num_scalar_prefetch=1,
            grid=(rows // tile,),
            in_specs=[row(ff), row(d), row(d), pl.BlockSpec(ext.shape, lambda i, m: (0, 0))]
            + [any_spec()] * chunk.count,
            out_specs=[row(d), row(d), row(d), pl.BlockSpec((1, d), lambda i, m: (0, 0))],
            scratch_shapes=[
                pltpu.VMEM((d, d), BF16),
                pltpu.VMEM((d, ff), BF16),
                pltpu.SemaphoreType.DMA((2 * copy_count(chunk),)),
            ],
        ),
        out_shape=[
            jax.ShapeDtypeStruct((rows, d), F32),
            jax.ShapeDtypeStruct((rows, d), BF16),
            jax.ShapeDtypeStruct((rows, d), BF16),
            jax.ShapeDtypeStruct((1, d), F32),
        ],
        compiler_params=params(),
        cost_estimate=cost(2 * rows * d * (d + ff), 14 * rows * d + 2 * rows * ff),
        name="mid_back",
    )(meta, din, middle, g, ext, *chunk.arrays)


def diagonal_sums(strip):
    for s in (64, 32, 16, 8):
        strip = strip[:s] + pltpu.roll(strip[s:], SPAN - s, 1)
    for s in (4, 2, 1):
        strip = strip + pltpu.roll(pltpu.roll(strip, 8 - s, 0), SPAN - s, 1)
    return strip[:1]


def attend_back_kernel(
    q_ref,
    k_ref,
    v_ref,
    do_ref,
    qaug_ref,
    kaug_ref,
    dist_ref,
    lse_ref,
    dq_ref,
    dk_ref,
    dv_ref,
    table_ref,
    strip_acc,
):
    pair = pl.program_id(0)
    lane = lax.broadcasted_iota(jnp.int32, (PAIR, 128), 1)
    q, k, v, do = q_ref[...], k_ref[...], v_ref[...], do_ref[...]
    qaug, kaug = qaug_ref[...], kaug_ref[...]
    k_turned = k.T
    strip_acc[...] = jnp.zeros_like(strip_acc)
    heads = []
    for hh in range(2):
        mine = (lane // 64) == hh
        heads.append(
            (
                jnp.where(mine, q, qaug),
                jnp.where(mine, k, kaug),
                jnp.where(mine, v, jnp.zeros_like(v)),
                k_turned[hh * 64 : (hh + 1) * 64, :],
                bias_strip(dist_ref[pl.ds(2 * pair + hh, 1), :]),
            )
        )
    for off, size in GROUPS:
        step = min(256, size)
        low = lax.broadcasted_iota(jnp.int32, (size, 128), 1) < 64
        dks, dvs = [None, None], [None, None]
        for i0 in range(0, size, step):
            lo, hi = off + i0, off + i0 + step
            dqs = []
            for hh in range(2):
                qa, ka, va, kt, strip = heads[hh]
                scores = dot_nt(ka[off : off + size], qa[lo:hi])
                bias = jnp.concatenate(
                    [
                        strip[:, (3 - t) * 128 + i0 : (3 - t) * 128 + i0 + step]
                        for t in range(size // 128)
                    ],
                    axis=0,
                )
                probs = jnp.exp(scores + bias - lse_ref[0, hh : hh + 1, lo:hi])
                d_probs = dot_nt(va[off : off + size], do[lo:hi])
                dv = dot(probs.astype(BF16), do[lo:hi])
                center = jnp.sum(probs * d_probs, axis=0, keepdims=True)
                d_scores = probs * (d_probs - center)
                for t in range(size // 128):
                    at = (3 - t) * 128 + i0
                    strip_acc[hh, :, at : at + step] += d_scores[t * 128 : (t + 1) * 128]
                ds_low = d_scores.astype(BF16)
                dk = dot(ds_low, q[lo:hi])
                dqs.append(dot(kt[:, off : off + size], ds_low))
                dks[hh] = dk if dks[hh] is None else dks[hh] + dk
                dvs[hh] = dv if dvs[hh] is None else dvs[hh] + dv
            dq_ref[lo:hi, :] = jnp.concatenate(dqs, axis=0).T.astype(BF16)
        dk_ref[off : off + size, :] = jnp.where(low, dks[0], dks[1]).astype(BF16)
        dv_ref[off : off + size, :] = jnp.where(low, dvs[0], dvs[1]).astype(BF16)

    place = (lax.broadcasted_iota(jnp.int32, (128, SPAN), 1) + 127) % SPAN
    row = lax.broadcasted_iota(jnp.int32, (128, SPAN), 0)
    chosen = (bucket_of(BLOCK - 1 - place) == row).astype(F32)
    sums = [diagonal_sums(strip_acc[hh]) for hh in range(2)]
    sums.append(jnp.zeros((6, SPAN), F32))
    found = lax.dot_general(
        jnp.concatenate(sums, axis=0),
        chosen,
        (((1,), (1,)), ((), ())),
        precision=lax.Precision.HIGHEST,
        preferred_element_type=F32,
    )

    @pl.when(pl.program_id(1) == 0)
    def _():
        table_ref[0] = found

    @pl.when(pl.program_id(1) > 0)
    def _():
        table_ref[0] += found


def attend_back_call(qkv, dctx, qaug, kaug, dist, lse):
    rows, d = dctx.shape
    pairs = rows // PAIR

    def part(t):
        return lambda h, p: (p, (h // 3) * 9 + t * 3 + h % 3)

    head = pl.BlockSpec((PAIR, 128), lambda h, p: (p, h))
    same = pl.BlockSpec((PAIR, 128), lambda h, p: (p, 0))
    grad = jax.ShapeDtypeStruct((rows, d), BF16)
    return pl.pallas_call(
        attend_back_kernel,
        grid=(H // 2, pairs),
        in_specs=[
            pl.BlockSpec((PAIR, 128), part(0)),
            pl.BlockSpec((PAIR, 128), part(1)),
            pl.BlockSpec((PAIR, 128), part(2)),
            head,
            same,
            same,
            pl.BlockSpec((16, SPAN), lambda h, p: (0, 0)),
            pl.BlockSpec((1, 2, PAIR), lambda h, p: (h, 0, p)),
        ],
        out_specs=[head, head, head, pl.BlockSpec((1, 8, 128), lambda h, p: (h, 0, 0))],
        out_shape=[grad, grad, grad, jax.ShapeDtypeStruct((H // 2, 8, 128), F32)],
        scratch_shapes=[pltpu.VMEM((2, 128, SPAN), F32)],
        compiler_params=params(),
        cost_estimate=cost(10 * pairs * H * 350000 * 128, 14 * rows * d, pairs * H * 350000),
        name="attend_back",
    )(qkv, qkv, qkv, dctx, qaug, kaug, dist, lse)


def in_back_kernel(chunk, meta, dq_ref, dk_ref, dv_ref, x_ref, dmid_ref, ext_ref, *rest):
    refs = rest[: chunk.count]
    dx_ref, gain_ref, w, sems = rest[chunk.count :]
    d = w.shape[0]

    @pl.when(pl.program_id(0) == 0)
    def _():
        run_copies(column_copies(chunk, meta, refs, 0, w.shape[1] // 2, w, sems))
        gain_ref[...] = jnp.zeros_like(gain_ref)

    h = d // 2
    parts = [r[:, s * h : (s + 1) * h] for s in range(2) for r in (dq_ref, dk_ref, dv_ref)]
    dn = dot_nt(jnp.concatenate(parts, axis=1), w[...])
    x = x_ref[...].astype(F32)
    scale = lax.rsqrt(jnp.mean(x * x, axis=-1, keepdims=True) + norm_eps)
    back, gain = norm_back(dn, x, ext_ref, 0, scale)
    gain_ref[...] += gain
    dx_ref[...] = dmid_ref[...] + back


def in_back_call(meta, dq, dk, dv, x, dmid, ext, chunk, tile=256):
    rows, d = x.shape
    row = lambda w: pl.BlockSpec((tile, w), lambda i, m: (i, 0))
    return pl.pallas_call(
        functools.partial(in_back_kernel, chunk),
        grid_spec=pltpu.PrefetchScalarGridSpec(
            num_scalar_prefetch=1,
            grid=(rows // tile,),
            in_specs=[row(d)] * 5
            + [pl.BlockSpec(ext.shape, lambda i, m: (0, 0))]
            + [any_spec()] * chunk.count,
            out_specs=[row(d), pl.BlockSpec((1, d), lambda i, m: (0, 0))],
            scratch_shapes=[
                pltpu.VMEM((d, 3 * d), BF16),
                pltpu.SemaphoreType.DMA((copy_count(chunk),)),
            ],
        ),
        out_shape=[
            jax.ShapeDtypeStruct((rows, d), F32),
            jax.ShapeDtypeStruct((1, d), F32),
        ],
        compiler_params=params(),
        cost_estimate=cost(6 * rows * d * d, 16 * rows * d + 6 * d * d),
        name="in_back",
    )(meta, dq, dk, dv, x, dmid, ext, *chunk.arrays)


def mask_lanes(lengths, rows):
    spot = jnp.arange(rows, dtype=jnp.int32)
    within = spot % PAIR
    first = jnp.array([0, 512, 768, 896, 960], jnp.int32)
    slot = jnp.sum((within[:, None] >= first[None, 1:]).astype(jnp.int32), axis=1)
    start = jnp.sum(jnp.where(slot[:, None] == jnp.arange(5)[None], first[None], 0), axis=1)
    docs = jnp.arange(lengths.shape[0], dtype=jnp.int32)
    document = spot // PAIR * 5 + slot
    own = jnp.sum(jnp.where(document[:, None] == docs[None], lengths[None], 0), axis=1)
    live = within - start < own
    late = slot == 4
    lane = jnp.arange(128, dtype=jnp.int32) % 64
    shown = [live & ~late, live & late]
    kaug = jnp.where(
        lane[None] == 0,
        jnp.where(shown[0], 0.0, MASKED)[:, None],
        jnp.where(lane[None] == 1, jnp.where(shown[1], 0.0, MASKED)[:, None], 0.0),
    ).astype(BF16)
    qaug = jnp.where(
        lane[None] == 0,
        jnp.where(late, 0.0, 1.0)[:, None],
        jnp.where(lane[None] == 1, jnp.where(late, 1.0, 0.0)[:, None], 0.0),
    ).astype(BF16)
    return qaug, kaug, live


def placed_rows(vector, me, rows):
    count = vector.shape[0]
    spot = jnp.arange(rows * 128, dtype=jnp.int32)[None] - me * count
    hit = spot == jnp.arange(count, dtype=jnp.int32)[:, None]
    flat = jnp.sum(jnp.where(hit, vector.astype(F32)[:, None], 0.0), axis=0)
    return flat.reshape(rows, 128)


def placed_table(vector, me):
    count = vector.shape[0]
    head = jnp.arange(16, dtype=jnp.int32)[:, None]
    bucket = jnp.arange(128, dtype=jnp.int32)[None]
    entry = jnp.where((head < H) & (bucket < BUCKETS), bucket * H + head, -1) - me * count
    hit = entry[None] == jnp.arange(count, dtype=jnp.int32)[:, None, None]
    return jnp.sum(jnp.where(hit, vector.astype(F32)[:, None, None], 0.0), axis=0)


def local(
    ring,
    hidden,
    gain_attn,
    rel_table,
    query_weight,
    key_weight,
    value_weight,
    output_weight,
    gain_ffn,
    inner_weight,
    outer_weight,
    lengths,
    cotangent,
):
    rows, d = hidden.shape
    ff = inner_weight.shape[1]
    n = ring.n
    shard_rows = query_weight.shape[0]
    outer_rows = outer_weight.shape[0]
    direct = shard_rows % 16 == 0 and shard_rows >= 32 and outer_rows % 32 == 0
    me = lax.axis_index("fsdp")
    core = lax.axis_index("dp")
    meta = ring.meta()
    h = d // 2

    def half(w, which):
        width = w.shape[1] // 2
        return lax.dynamic_slice_in_dim(w, which * width, width, 1)

    small = jnp.concatenate(
        [
            placed_rows(gain_attn, me, d // 128),
            placed_rows(gain_ffn, me, d // 128),
            jnp.zeros((16 - 2 * (d // 128), 128), F32),
            placed_table(rel_table, me),
        ],
        axis=0,
    ).astype(BF16)
    pack_a = [half(w, core) for w in (query_weight, key_weight, value_weight)]
    if direct:
        pack_a.append(jnp.pad(small, ((0, shard_rows - 32), (0, 0))))
    pack_a = jnp.concatenate(pack_a, axis=1)
    pack_b = jnp.concatenate([half(output_weight, core), half(inner_weight, core)], axis=1)
    pack_c = lax.dynamic_slice_in_dim(
        outer_weight, core * (outer_rows // 2), outer_rows // 2, 0
    )

    def whole_columns(own, rec):
        both = []
        for parts, first in ((own, core == 0), (rec, core == 1)):
            pieces = ring.to_origin(jnp.concatenate(parts, axis=0), first)
            both.append(pieces.reshape(-1, pieces.shape[2]))
        first = jnp.where(core == 0, both[0], both[1])
        second = jnp.where(core == 0, both[1], both[0])
        return jnp.stack([first, second])

    got_a = gather_pieces(ring, pack_a)
    got_b = gather_pieces(ring, pack_b)
    got_c = gather_pieces(ring, pack_c)
    if direct:
        chunk_a, chunk_b, chunk_c = (Pieces(*g, n) for g in (got_a, got_b, got_c))
        ext = sum(jnp.sum(p[:, :32, 3 * h :].astype(F32), axis=0) for p in got_a[0])
    else:
        chunk_a = Whole(whole_columns(*got_a))
        chunk_b = Whole(whole_columns(*got_b))
        both = [
            ring.to_origin(jnp.concatenate(parts, axis=0), first)
            for parts, first in zip(got_c, (core == 0, core == 1))
        ]
        first = jnp.where(core == 0, both[0], both[1])
        second = jnp.where(core == 0, both[1], both[0])
        chunk_c = Whole(jnp.stack([first, second], axis=1).reshape(ff, d))
        ext = lax.psum(small.astype(F32), "fsdp")

    qaug, kaug, live = mask_lanes(lengths, rows)
    g = jnp.where(live[:, None], cotangent, jnp.zeros_like(cotangent))

    qkv, normed, dist = qkv_call(meta, hidden, ext, chunk_a)
    ctx, lse = attend_call(qkv, qaug, kaug, dist)
    middle, normed2, act, slope = mid_call(meta, ctx, hidden, ext, chunk_b, ff)

    def split_columns(a, bs, steps, name, extra=None):
        if direct:
            return column_grad_call(meta, a, bs, n, steps, name, extra)
        full = [jnp.einsum("td,tf->df", a, b, preferred_element_type=F32) for b in bs]
        out = []
        for which in (core, 1 - core):
            part = jnp.concatenate([half(w, which) for w in full], axis=1).astype(BF16)
            part = part.reshape(n, d // n, part.shape[1])
            out.append(ring.from_origin(part, which == 0))
        return out

    def split_rows(a, b):
        if direct:
            return outer_grad_call(meta, a, b, n)
        full = jnp.einsum("tf,td->fd", a, b, preferred_element_type=F32).astype(BF16)
        full = full.reshape(n, 2, outer_rows // 2, d)
        return [
            ring.from_origin(
                lax.dynamic_index_in_dim(full, which, 1, keepdims=False), which == 0
            )
            for which in (core, 1 - core)
        ]

    sum_c = reduce_pieces(ring, *split_rows(act, g))
    result, d_inner = out_call(meta, act, middle, g, slope, chunk_c)
    sum_b = reduce_pieces(ring, *split_columns(normed2, [d_inner], 3, "inner_grad"))
    d_middle, d_att, d_ctx, grad_gain_f = mid_back_call(meta, d_inner, middle, g, ext, chunk_b)
    sum_o = reduce_pieces(ring, *split_columns(ctx, [d_att], 1, "output_grad"))
    dq, dk, dv, found = attend_back_call(qkv, d_ctx, qaug, kaug, dist, lse)
    grad_hidden, grad_gain_a = in_back_call(meta, dq, dk, dv, hidden, d_middle, ext, chunk_a)
    extra = jnp.concatenate(
        [
            grad_gain_a.reshape(d // 128, 128),
            grad_gain_f.reshape(d // 128, 128),
            jnp.zeros((16 - 2 * (d // 128), 128), F32),
            found[:, :2].reshape(H, 128),
            jnp.zeros((4, 128), F32),
        ],
        axis=0,
    )
    if direct:
        block = jnp.pad(extra, ((0, shard_rows - 32), (0, 0))).astype(BF16)
        sum_a = reduce_pieces(ring, *split_columns(normed, [dq, dk, dv], 1, "qkv_grad", block))
        extra = sum_a[:32, 3 * h :]
    else:
        sum_a = reduce_pieces(ring, *split_columns(normed, [dq, dk, dv], 1, "qkv_grad"))
        extra = lax.psum(extra, ("dp", "fsdp"))

    own = [sum_a[:, : 3 * h], sum_o, sum_b, sum_c]
    other = [shift(s, ring.swap_core()) for s in own]
    low = [jnp.where(core == 0, a, b) for a, b in zip(own, other)]
    high = [jnp.where(core == 0, b, a) for a, b in zip(own, other)]
    grads = [
        jnp.concatenate([low[0][:, t * h : (t + 1) * h], high[0][:, t * h : (t + 1) * h]], axis=1)
        for t in range(3)
    ]
    grad_output = jnp.concatenate([low[1], high[1]], axis=1)
    grad_inner = jnp.concatenate([low[2], high[2]], axis=1)
    grad_outer = jnp.concatenate([low[3], high[3]], axis=0)
    per = d // n
    gain_a = lax.dynamic_slice_in_dim(extra[: d // 128].reshape(-1), me * per, per, 0)
    gain_f = lax.dynamic_slice_in_dim(
        extra[d // 128 : 2 * (d // 128)].reshape(-1), me * per, per, 0
    )
    table = extra[16 : 16 + H, :BUCKETS].T.reshape(-1)
    table = lax.dynamic_slice_in_dim(table, me * rel_table.shape[0], rel_table.shape[0], 0)
    return (
        result,
        grad_hidden,
        gain_a,
        table,
        grads[0],
        grads[1],
        grads[2],
        grad_output,
        gain_f,
        grad_inner,
        grad_outer,
    )


def solution(mesh):
    both = P(("dp", "fsdp"), None)
    line = P("fsdp")
    wide = P("fsdp", None)
    in_specs = (both, line, line, wide, wide, wide, wide, line, wide, wide, P(("dp", "fsdp")), both)
    out_specs = (both, both, line, line, wide, wide, wide, wide, line, wide, wide)
    return jax.shard_map(
        functools.partial(local, Ring(mesh)),
        mesh=mesh,
        in_specs=in_specs,
        out_specs=out_specs,
        check_vma=False,
    )
```

time: 1540 us -> 369 us (0.24)
  waiting for transfers between devices: 859 us -> 116 us
  local copies, waits for them, and re-layouts: 279 us -> 7.3 us
  matrix products: 178 us -> 0 us
  Pallas kernels: 0 us -> 169 us
  blocking collectives: 124 us -> 0 us
  starting transfers between devices: 0.51 us -> 42 us
  other arithmetic: 63.4 us -> 31.5 us
  between operations: 17.7 us -> 1.24 us
    reduce_scatter x6 -> x0, waiting for transfers between devices: 636 us -> none  [the longest x1 177 us: local(): lax.psum_scatter(summed[8], 'fsdp', scatter_dimension=0, tiled=True)]
    dot_general x34 -> x0, matrix products: 178 us -> none  [the longest x4 32.4 us: masked_scores(): jnp.einsum('ihd,jhd->hij', block_query, block_key, preferred_element_type...]
    pallas_call x0 -> x11, Pallas kernels: none -> 169 us  [the longest x1 33.1 us: attend_back_call(): pl.pallas_call(attend_back_kernel, grid=(H // 2, pairs), in_specs=[pl.Blo...]
    all_gather x6 -> x0, waiting for transfers between devices: 168 us -> none  [the longest x1 76.5 us: local(): lax.all_gather(inner_weight, 'fsdp', axis=0, tiled=True)]
    unnamed x2 -> x0, blocking collectives: 122 us -> none
    ppermute x0 -> x42, waiting for transfers between devices: none -> 116 us  [shift(): return lax.ppermute(value, ('dp', 'fsdp'), pairs)]
    reshape x41 -> x3, local copies, waits for them, and re-layouts: 99.7 us -> 0.13 us  [the longest x1 0.1 us: local(): table = extra[16:16 + H, :BUCKETS].T.reshape(-1)]
    psum x1 -> x0, waiting for transfers between devices: 51.8 us -> none  [local(): lax.psum(grad_query.astype(jnp.bfloat16), 'dp').astype(jnp.float32)]
  transfers between devices with their start and end apart: 13 -> 42, of which waited for: 10 -> 21; matrix products, arithmetic and copies ran while one was open for 22% -> 9% of each run, Pallas kernels for 0% -> 23%
where the time goes in v1:
time: 369 us; the launch traced here: 368 us
  Pallas kernels  169 us (46%)
  waiting for transfers between devices  116 us (31%)
  starting transfers between devices  42 us (11%)
  other arithmetic  31.5 us (9%)
  local copies, waits for them, and re-layouts  7.3 us (2%)
    ppermute x42, waiting for transfers between devices, shift(): return lax.ppermute(value, ('dp', 'fsdp'), pairs)  116 us
    ppermute x42, starting transfers between devices, shift(): return lax.ppermute(value, ('dp', 'fsdp'), pairs)  42 us
    pallas_call x1, Pallas kernels, attend_back_call(): pl.pallas_call(attend_back_kernel, grid=(H // 2, pairs), in_specs=[pl.Blo...  33.1 us
    pallas_call x3, Pallas kernels, column_grad_call(): pl.pallas_call(functools.partial(column_grad_kernel, n, steps, extra is n...  28.4 us
    pallas_call x1, Pallas kernels, mid_call(): pl.pallas_call(functools.partial(mid_kernel, chunk), grid_spec=grid_spec,...  20.5 us
    pallas_call x1, Pallas kernels, attend_call(): pl.pallas_call(attend_kernel, grid=(pairs, H // 2), in_specs=[pl.BlockSpe...  19.8 us
    pallas_call x1, Pallas kernels, out_call(): pl.pallas_call(functools.partial(out_kernel, chunk), grid_spec=pltpu.Pref...  17.8 us
    pallas_call x1, Pallas kernels, mid_back_call(): pl.pallas_call(functools.partial(mid_back_kernel, chunk), grid_spec=pltpu...  17.2 us
  transfers between devices with their start and end apart: 42, of which 21 were waited for; matrix products, arithmetic and copies ran while one was open for 9% of the time, Pallas kernels for 23%

profile of v1, /device:TPU:0, one launch (start us, length us, event | category | flops | bytes accessed | tf_op | source)
XLA Modules:
  0.0 367.6 jit_solution(1357137388723858920)
XLA Ops:
  1.7 4.1 %collective-permute-start.6 = (bf16[1,48,1920]{2,1,0:T(8,128)(2,1)S(1)}, bf16[1,48,1920]{2,1,0:T(8,128)(2,1)S(1)}, u32[]{:S(2)}, u32[]{:S(2)}) collective-permute-start(bf16[1,48,1920]{2,1,0:T(8,128)(2,1)S(1)} %maximum_bitcast_fusion), channel_id=1, source_target_pairs={{0,8},{1,9},{2,10},{3,11},{4,12},{5,13},{6,14},{7,15},{8,0},{9,1},... | collective-permute-start | bytes 552968 | tf_op jit(solution)/shard_map/ppermute | solution.py:128
  8.8 5.5 %collective-permute-done.6 = bf16[1,48,1920]{2,1,0:T(8,128)(2,1)S(1)} collective-permute-done((bf16[1,48,1920]{2,1,0:T(8,128)(2,1)S(1)}, bf16[1,48,1920]{2,1,0:T(8,128)(2,1)S(1)}, u32[]{:S(2)}, u32[]{:S(2)}) %collective-permute-start.6) | collective-permute-done | bytes 184352 | tf_op jit(solution)/shard_map/ppermute | solution.py:128
  18.7 8.2 %collective-permute-done.7 = bf16[2,48,1920]{2,1,0:T(8,128)(2,1)S(1)} collective-permute-done((bf16[2,48,1920]{2,1,0:T(8,128)(2,1)S(1)}, bf16[2,48,1920]{2,1,0:T(8,128)(2,1)S(1)}, u32[]{:S(2)}, u32[]{:S(2)}) %collective-permute-start.7) | collective-permute-done | bytes 368672 | tf_op jit(solution)/shard_map/ppermute | solution.py:128
  47.6 8.9 %collective-permute-done.2 = bf16[4,48,1280]{2,1,0:T(8,128)(2,1)} collective-permute-done((bf16[4,48,1280]{2,1,0:T(8,128)(2,1)}, bf16[4,48,1280]{2,1,0:T(8,128)(2,1)}, u32[]{:S(2)}, u32[]{:S(2)}) %collective-permute-start.2) | collective-permute-done | bytes 491552 | tf_op jit(solution)/shard_map/ppermute | solution.py:128
  59.6 9.5 %collective-permute-done.14 = bf16[4,96,768]{2,1,0:T(8,128)(2,1)S(1)} collective-permute-done((bf16[4,96,768]{2,1,0:T(8,128)(2,1)S(1)}, bf16[4,96,768]{2,1,0:T(8,128)(2,1)S(1)}, u32[]{:S(2)}, u32[]{:S(2)}) %collective-permute-start.14) | collective-permute-done | bytes 589856 | tf_op jit(solution)/shard_map/ppermute | solution.py:128
  72.5 7.5 %collective-permute-done.3.rest_1_ = bf16[8,48,1280]{2,1,0:T(8,128)(2,1)} collective-permute-done((bf16[8,48,1280]{2,1,0:T(8,128)(2,1)}, bf16[8,48,1280]{2,1,0:T(8,128)(2,1)}, u32[]{:S(2)}, u32[]{:S(2)}) %collective-permute-start.3) | collective-permute-done | bytes 983072 | tf_op jit(solution)/shard_map/ppermute | solution.py:128
  85.4 7.3 %collective-permute-done.15.rest_1_ = bf16[8,96,768]{2,1,0:T(8,128)(2,1)} collective-permute-done((bf16[8,96,768]{2,1,0:T(8,128)(2,1)}, bf16[8,96,768]{2,1,0:T(8,128)(2,1)}, u32[]{:S(2)}, u32[]{:S(2)}) %collective-permute-start.15) | collective-permute-done | bytes 1179680 | tf_op jit(solution)/shard_map/ppermute | solution.py:128
  94.3 10.1 %qkv.1 = (bf16[1024,2304]{1,0:T(8,128)(2,1)}, bf16[1024,768]{1,0:T(8,128)(2,1)}, f32[16,1024]{1,0:T(8,128)}) custom-call(s32[65]{0:T(128)} %concatenate.68.meta, bf16[1024,768]{1,0:T(8,128)(2,1)} %x_ref.5, f32[32,128]{1,0:T(8,128)} %add.219.ext_ref, bf16[8,48,1280]{2,1,0:T(8,128)(2,1)} %pad_maximum_fusion.2.rest_0_, ...), custom_call_target="tpu_custom_call" | custom-call | flops 3623878656 | bytes 14548992 | tf_op jit(solution)/shard_map/qkv/pallas_call | solution.py:310
  104.4 19.8 %attend.1 = (bf16[1024,768]{1,0:T(8,128)(2,1)}, f32[6,2,1024]{2,1,0:T(2,128)}) custom-call(bf16[1024,2304]{1,0:T(8,128)(2,1)} %get-tuple-element.40.q_ref.k_ref.v_ref, bf16[1024,2304]{1,0:T(8,128)(2,1)} %get-tuple-element.40.q_ref.k_ref.v_ref, bf16[1024,2304]{1,0:T(8,128)(2,1)} %get-tuple-element.40.q_ref.k_ref.v_ref, ...), custom_call_target="tpu_custom_call" | custom-call | flops 2150400000 | bytes 6291456 | tf_op jit(solution)/shard_map/attend/pallas_call | solution.py:379
  124.2 20.5 %mid.1 = (f32[1024,768]{1,0:T(8,128)}, bf16[1024,768]{1,0:T(8,128)(2,1)}, bf16[1024,3072]{1,0:T(8,128)(2,1)}, bf16[1024,3072]{1,0:T(8,128)(2,1)}) custom-call(s32[65]{0:T(128)} %concatenate.68.meta, bf16[1024,768]{1,0:T(8,128)(2,1)} %get-tuple-element.42.ctx_ref.a_ref, bf16[1024,768]{1,0:T(8,128)(2,1)} %x_ref.5, f32[32,128]{1,0:T(8,128)} %add.219.ext_ref, ...), custom_call_target="tpu_custom_call" | custom-call | flops 6039797760 | bytes 20447232 | tf_op jit(solution)/shard_map/mid/pallas_call | solution.py:458
  146.1 17.8 %out.1 = (f32[1024,768]{1,0:T(8,128)}, bf16[1024,3072]{1,0:T(8,128)(2,1)}) custom-call(s32[65]{0:T(128)} %concatenate.68.meta, bf16[1024,3072]{1,0:T(8,128)(2,1)} %get-tuple-element.43.act_ref, f32[1024,768]{1,0:T(8,128)} %get-tuple-element.44.mid_ref, bf16[1024,768]{1,0:T(8,128)(2,1)} %broadcast_select_fusion.g_ref, ...), custom_call_target="tpu_custom_call" | custom-call | flops 9663676416 | bytes 26738688 | tf_op jit(solution)/shard_map/out/pallas_call | solution.py:529
  163.9 17.2 %mid_back.1 = (f32[1024,768]{1,0:T(8,128)}, bf16[1024,768]{1,0:T(8,128)(2,1)}, bf16[1024,768]{1,0:T(8,128)(2,1)}, f32[1,768]{1,0:T(1,128)}) custom-call(s32[65]{0:T(128)} %concatenate.68.meta, bf16[1024,3072]{1,0:T(8,128)(2,1)} %get-tuple-element.47.din_ref.rest_0_, f32[1024,768]{1,0:T(8,128)} %get-tuple-element.44.mid_ref, ...), custom_call_target="tpu_custom_call" | custom-call | flops 6039797760 | bytes 17301504 | tf_op jit(solution)/shard_map/mid_back/pallas_call | solution.py:671
  181.1 6.1 %output_grad.1 = (bf16[16,48,384]{2,1,0:T(8,128)(2,1)}, bf16[16,48,384]{2,1,0:T(8,128)(2,1)}) custom-call(s32[65]{0:T(128)} %concatenate.68.meta, bf16[1024,768]{1,0:T(8,128)(2,1)} %get-tuple-element.42.ctx_ref.a_ref, bf16[1024,768]{1,0:T(8,128)(2,1)} %get-tuple-element.61.rest_0_), custom_call_target="tpu_custom_call" | custom-call | flops 1207959552 | bytes 4325376 | tf_op jit(solution)/shard_map/output_grad/pallas_call | solution.py:603
  187.1 33.1 %attend_back.1 = (bf16[1024,768]{1,0:T(8,128)(2,1)}, bf16[1024,768]{1,0:T(8,128)(2,1)}, bf16[1024,768]{1,0:T(8,128)(2,1)}, f32[6,8,128]{2,1,0:T(8,128)}) custom-call(bf16[1024,2304]{1,0:T(8,128)(2,1)} %get-tuple-element.40.q_ref.k_ref.v_ref, bf16[1024,2304]{1,0:T(8,128)(2,1)} %get-tuple-element.40.q_ref.k_ref.v_ref, ...), custom_call_target="tpu_custom_call" | custom-call | flops 5376000000 | bytes 11010048 | tf_op jit(solution)/shard_map/attend_back/pallas_call | solution.py:804
  221.0 11.8 %in_back.1 = (f32[1024,768]{1,0:T(8,128)}, f32[1,768]{1,0:T(1,128)}) custom-call(s32[65]{0:T(128)} %concatenate.68.meta, bf16[1024,768]{1,0:T(8,128)(2,1)} %get-tuple-element.50.dq_ref.rest_0_, bf16[1024,768]{1,0:T(8,128)(2,1)} %get-tuple-element.51.dk_ref.rest_1_, bf16[1024,768]{1,0:T(8,128)(2,1)} %get-tuple-element.52.dv_ref.rest_2_, ...), custom_call_target="tpu_custom_call" | custom-call | flops 3623878656 | bytes 16121856 | tf_op jit(solution)/shard_map/in_back/pallas_call | solution.py:849
  234.7 10.9 %qkv_grad.1 = (bf16[16,48,1280]{2,1,0:T(8,128)(2,1)}, bf16[16,48,1280]{2,1,0:T(8,128)(2,1)}) custom-call(s32[65]{0:T(128)} %concatenate.68.meta, bf16[1024,768]{1,0:T(8,128)(2,1)} %get-tuple-element.55.a_ref, bf16[1024,768]{1,0:T(8,128)(2,1)} %get-tuple-element.50.dq_ref.rest_0_, bf16[1024,768]{1,0:T(8,128)(2,1)} %get-tuple-element.51.dk_ref.rest_1_, ...), custom_call_target="tpu_custom_call" | custom-call | flops 3623878656 | bytes 9830400 | tf_op jit(solution)/shard_map/qkv_grad/pallas_call | solution.py:603
  245.7 11.5 %inner_grad.1 = (bf16[16,48,1536]{2,1,0:T(8,128)(2,1)}, bf16[16,48,1536]{2,1,0:T(8,128)(2,1)}) custom-call(s32[65]{0:T(128)} %concatenate.68.meta, bf16[1024,768]{1,0:T(8,128)(2,1)} %get-tuple-element.64.a_ref, bf16[1024,3072]{1,0:T(8,128)(2,1)} %get-tuple-element.47.din_ref.rest_0_), custom_call_target="tpu_custom_call" | custom-call | flops 4831838208 | bytes 12582912 | tf_op jit(solution)/shard_map/inner_grad/pallas_call | solution.py:603
  258.9 5.6 %collective-permute-done.25 = bf16[8,48,384]{2,1,0:T(8,128)(2,1)S(1)} collective-permute-done((bf16[8,48,384]{2,1,0:T(8,128)(2,1)S(1)}, bf16[8,48,384]{2,1,0:T(8,128)(2,1)S(1)}, u32[]{:S(2)}, u32[]{:S(2)}) %collective-permute-start.25) | collective-permute-done | bytes 294944 | tf_op jit(solution)/shard_map/ppermute | solution.py:128
  266.2 10.7 %outer_grad.1 = (bf16[16,96,768]{2,1,0:T(8,128)(2,1)}, bf16[16,96,768]{2,1,0:T(8,128)(2,1)}) custom-call(s32[65]{0:T(128)} %concatenate.68.meta, bf16[1024,3072]{1,0:T(8,128)(2,1)} %get-tuple-element.43.act_ref, bf16[1024,768]{1,0:T(8,128)(2,1)} %broadcast_select_fusion.g_ref), custom_call_target="tpu_custom_call" | custom-call | flops 4831838208 | bytes 12582912 | tf_op jit(solution)/shard_map/outer_grad/pallas_call | solution.py:491
  302.6 9.5 %collective-permute-done.20 = bf16[4,48,1280]{2,1,0:T(8,128)(2,1)S(1)} collective-permute-done((bf16[4,48,1280]{2,1,0:T(8,128)(2,1)S(1)}, bf16[4,48,1280]{2,1,0:T(8,128)(2,1)S(1)}, u32[]{:S(2)}, u32[]{:S(2)}) %collective-permute-start.20) | collective-permute-done | bytes 491552 | tf_op jit(solution)/shard_map/ppermute | solution.py:128
  321.3 11.7 %collective-permute-done.37 = bf16[8,96,768]{2,1,0:T(8,128)(2,1)S(1)} collective-permute-done((bf16[8,96,768]{2,1,0:T(8,128)(2,1)S(1)}, bf16[8,96,768]{2,1,0:T(8,128)(2,1)S(1)}, u32[]{:S(2)}, u32[]{:S(2)}) %collective-permute-start.37) | collective-permute-done | bytes 1179680 | tf_op jit(solution)/shard_map/ppermute | solution.py:128
  338.6 5.6 %collective-permute-done.38 = bf16[4,96,768]{2,1,0:T(8,128)(2,1)S(1)} collective-permute-done((bf16[4,96,768]{2,1,0:T(8,128)(2,1)}, bf16[4,96,768]{2,1,0:T(8,128)(2,1)S(1)}, u32[]{:S(2)}, u32[]{:S(2)}) %collective-permute-start.38) | collective-permute-done | bytes 589856 | tf_op jit(solution)/shard_map/ppermute | solution.py:128
  349.9 6.6 %collective-permute-done.39 = bf16[2,96,768]{2,1,0:T(8,128)(2,1)S(1)} collective-permute-done((bf16[2,96,768]{2,1,0:T(8,128)(2,1)S(1)}, bf16[2,96,768]{2,1,0:T(8,128)(2,1)S(1)}, u32[]{:S(2)}, u32[]{:S(2)}) %collective-permute-start.39) | collective-permute-done | bytes 294944 | tf_op jit(solution)/shard_map/ppermute | solution.py:128
  357.6 7.3 %collective-permute-done.40 = bf16[1,96,768]{2,1,0:T(8,128)(2,1)S(1)} collective-permute-done((bf16[1,96,768]{2,1,0:T(8,128)(2,1)S(1)}, bf16[1,96,768]{2,1,0:T(8,128)(2,1)S(1)}, u32[]{:S(2)}, u32[]{:S(2)}) %collective-permute-start.40) | collective-permute-done | bytes 147488 | tf_op jit(solution)/shard_map/ppermute | solution.py:128
  (198 shorter events, 99.6 us)
Async XLA Ops:
  1.7 12.7 %collective-permute-start.6 = (bf16[1,48,1920]{2,1,0:T(8,128)(2,1)S(1)}, bf16[1,48,1920]{2,1,0:T(8,128)(2,1)S(1)}, u32[]{:S(2)}, u32[]{:S(2)}) collective-permute-start(bf16[1,48,1920]{2,1,0:T(8,128)(2,1)S(1)} %maximum_bitcast_fusion), channel_id=1, source_target_pairs={{0,8},{1,9},{2,10},{3,11},{4,12},{5,13},{6,14},{7,15},{8,0},{9,1},... | collective-permute-start | bytes 552968 | tf_op jit(solution)/shard_map/ppermute | solution.py:128
  15.3 15.7 %collective-permute-start = (bf16[1,48,1280]{2,1,0:T(8,128)(2,1)S(1)}, bf16[1,48,1280]{2,1,0:T(8,128)(2,1)S(1)}, u32[]{:S(2)}, u32[]{:S(2)}) collective-permute-start(bf16[1,48,1280]{2,1,0:T(8,128)(2,1)S(1)} %maximum_bitcast_fusion.1), channel_id=1, source_target_pairs={{0,8},{1,9},{2,10},{3,11},{4,12},{5,13},{6,14},{7,15},{8,0},{9,1},... | collective-permute-start | bytes 368648 | tf_op jit(solution)/shard_map/ppermute | solution.py:128
  27.0 15.1 %collective-permute-start.8 = (bf16[4,48,1920]{2,1,0:T(8,128)(2,1)S(1)}, bf16[4,48,1920]{2,1,0:T(8,128)(2,1)S(1)}, u32[]{:S(2)}, u32[]{:S(2)}) collective-permute-start(bf16[4,48,1920]{2,1,0:T(8,128)(2,1)S(1)} %pad_maximum_fusion.3), channel_id=1, source_target_pairs={{0,2},{1,3},{2,0},{3,1},{4,6},{5,7},{6,4},{7,5},{8,10},{9,11},{10,... | collective-permute-start | bytes 2211848 | tf_op jit(solution)/shard_map/ppermute | solution.py:128
  42.0 14.5 %collective-permute-start.2 = (bf16[4,48,1280]{2,1,0:T(8,128)(2,1)}, bf16[4,48,1280]{2,1,0:T(8,128)(2,1)}, u32[]{:S(2)}, u32[]{:S(2)}) collective-permute-start(bf16[4,48,1280]{2,1,0:T(8,128)(2,1)} %pad_maximum_fusion.7), channel_id=1, source_target_pairs={{0,2},{1,3},{2,0},{3,1},{4,6},{5,7},{6,4},{7,5},{8,10},{9,11},{10,... | collective-permute-start | bytes 1474568 | tf_op jit(solution)/shard_map/ppermute | solution.py:128
  42.2 38.2 %collective-permute-start.9 = (bf16[8,48,1920]{2,1,0:T(8,128)(2,1)S(1)}, bf16[8,48,1920]{2,1,0:T(8,128)(2,1)}, u32[]{:S(2)}, u32[]{:S(2)}) collective-permute-start(bf16[8,48,1920]{2,1,0:T(8,128)(2,1)S(1)} %pad_maximum_fusion.rest_0_), channel_id=1, source_target_pairs={{0,1},{1,0},{2,3},{3,2},{4,5},{5,4},{6,7},{7,6},{8,9},{9,8},{10,11... | collective-permute-start | bytes 4423688 | tf_op jit(solution)/shard_map/ppermute | solution.py:128
  46.2 22.8 %collective-permute-start.14 = (bf16[4,96,768]{2,1,0:T(8,128)(2,1)S(1)}, bf16[4,96,768]{2,1,0:T(8,128)(2,1)S(1)}, u32[]{:S(2)}, u32[]{:S(2)}) collective-permute-start(bf16[4,96,768]{2,1,0:T(8,128)(2,1)S(1)} %pad_maximum_fusion.4), channel_id=1, source_target_pairs={{0,2},{1,3},{2,0},{3,1},{4,6},{5,7},{6,4},{7,5},{8,10},{9,11},{10,... | collective-permute-start | bytes 1769480 | tf_op jit(solution)/shard_map/ppermute | solution.py:128
  58.6 21.4 %collective-permute-start.3 = (bf16[8,48,1280]{2,1,0:T(8,128)(2,1)}, bf16[8,48,1280]{2,1,0:T(8,128)(2,1)}, u32[]{:S(2)}, u32[]{:S(2)}) collective-permute-start(bf16[8,48,1280]{2,1,0:T(8,128)(2,1)} %pad_maximum_fusion.2.rest_0_), channel_id=1, source_target_pairs={{0,1},{1,0},{2,3},{3,2},{4,5},{5,4},{6,7},{7,6},{8,9},{9,8},{10,11... | collective-permute-start | bytes 2949128 | tf_op jit(solution)/shard_map/ppermute | solution.py:128
  71.1 21.5 %collective-permute-start.15 = (bf16[8,96,768]{2,1,0:T(8,128)(2,1)}, bf16[8,96,768]{2,1,0:T(8,128)(2,1)}, u32[]{:S(2)}, u32[]{:S(2)}) collective-permute-start(bf16[8,96,768]{2,1,0:T(8,128)(2,1)} %pad_maximum_fusion.1.rest_0_), channel_id=1, source_target_pairs={{0,1},{1,0},{2,3},{3,2},{4,5},{5,4},{6,7},{7,6},{8,9},{9,8},{10,11... | collective-permute-start | bytes 3538952 | tf_op jit(solution)/shard_map/ppermute | solution.py:128
  71.9 13.0 %collective-permute-start.4 = (bf16[8,48,1280]{2,1,0:T(8,128)(2,1)}, bf16[8,48,1280]{2,1,0:T(8,128)(2,1)}, u32[]{:S(2)}, u32[]{:S(2)}) collective-permute-start(bf16[8,48,1280]{2,1,0:T(8,128)(2,1)} %pad_maximum_fusion.2.rest_0_), channel_id=1, source_target_pairs={{0,16},{1,17},{2,18},{3,19},{4,20},{5,21},{6,22},{7,23},{8,24},{9,... | collective-permute-start | bytes 2949128 | tf_op jit(solution)/shard_map/ppermute | solution.py:128
  72.0 52.2 %collective-permute-start.10 = (bf16[8,48,1920]{2,1,0:T(8,128)(2,1)S(1)}, bf16[8,48,1920]{2,1,0:T(8,128)(2,1)}, u32[]{:S(2)}, u32[]{:S(2)}) collective-permute-start(bf16[8,48,1920]{2,1,0:T(8,128)(2,1)S(1)} %pad_maximum_fusion.rest_0_), channel_id=1, source_target_pairs={{0,16},{1,17},{2,18},{3,19},{4,20},{5,21},{6,22},{7,23},{8,24},{9,... | collective-permute-start | bytes 4423688 | tf_op jit(solution)/shard_map/ppermute | solution.py:128
  80.0 14.2 %collective-permute-start.5 = (bf16[8,48,1280]{2,1,0:T(8,128)(2,1)}, bf16[8,48,1280]{2,1,0:T(8,128)(2,1)}, u32[]{:S(2)}, u32[]{:S(2)}) collective-permute-start(bf16[8,48,1280]{2,1,0:T(8,128)(2,1)} %collective-permute-done.3.rest_1_), channel_id=1, source_target_pairs={{0,16},{1,17},{2,18},{3,19},{4,20},{5,21},{6,22},{7,23},{8,24},{9,... | collective-permute-start | bytes 2949128 | tf_op jit(solution)/shard_map/ppermute | solution.py:128
  80.5 43.7 %collective-permute-start.11 = (bf16[8,48,1920]{2,1,0:T(8,128)(2,1)}, bf16[8,48,1920]{2,1,0:T(8,128)(2,1)}, u32[]{:S(2)}, u32[]{:S(2)}) collective-permute-start(bf16[8,48,1920]{2,1,0:T(8,128)(2,1)} %collective-permute-done.9.rest_1_), channel_id=1, source_target_pairs={{0,16},{1,17},{2,18},{3,19},{4,20},{5,21},{6,22},{7,23},{8,24},{9,... | collective-permute-start | bytes 4423688 | tf_op jit(solution)/shard_map/ppermute | solution.py:128
  84.9 59.8 %collective-permute-start.16 = (bf16[8,96,768]{2,1,0:T(8,128)(2,1)}, bf16[8,96,768]{2,1,0:T(8,128)(2,1)S(1)}, u32[]{:S(2)}, u32[]{:S(2)}) collective-permute-start(bf16[8,96,768]{2,1,0:T(8,128)(2,1)} %pad_maximum_fusion.1.rest_0_), channel_id=1, source_target_pairs={{0,16},{1,17},{2,18},{3,19},{4,20},{5,21},{6,22},{7,23},{8,24},{9,... | collective-permute-start | bytes 3538952 | tf_op jit(solution)/shard_map/ppermute | solution.py:128
  92.7 52.0 %collective-permute-start.17 = (bf16[8,96,768]{2,1,0:T(8,128)(2,1)}, bf16[8,96,768]{2,1,0:T(8,128)(2,1)S(1)}, u32[]{:S(2)}, u32[]{:S(2)}) collective-permute-start(bf16[8,96,768]{2,1,0:T(8,128)(2,1)} %collective-permute-done.15.rest_1_), channel_id=1, source_target_pairs={{0,16},{1,17},{2,18},{3,19},{4,20},{5,21},{6,22},{7,23},{8,24},{9,... | collective-permute-start | bytes 3538952 | tf_op jit(solution)/shard_map/ppermute | solution.py:128
  234.3 23.2 %collective-permute-start.24 = (bf16[16,48,384]{2,1,0:T(8,128)(2,1)S(1)}, bf16[16,48,384]{2,1,0:T(8,128)(2,1)S(1)}, u32[]{:S(2)}, u32[]{:S(2)}) collective-permute-start(bf16[16,48,384]{2,1,0:T(8,128)(2,1)S(1)} %copy-done.18), channel_id=1, source_target_pairs={{0,16},{1,17},{2,18},{3,19},{4,20},{5,21},{6,22},{7,23},{8,24},{9,... | collective-permute-start | bytes 1769480 | tf_op jit(solution)/shard_map/ppermute | solution.py:128
  245.6 33.2 %collective-permute-start.18 = (bf16[16,48,1280]{2,1,0:T(8,128)(2,1)}, bf16[16,48,1280]{2,1,0:T(8,128)(2,1)}, u32[]{:S(2)}, u32[]{:S(2)}) collective-permute-start(bf16[16,48,1280]{2,1,0:T(8,128)(2,1)} %get-tuple-element.60), channel_id=1, source_target_pairs={{0,16},{1,17},{2,18},{3,19},{4,20},{5,21},{6,22},{7,23},{8,24},{9,... | collective-permute-start | bytes 5898248 | tf_op jit(solution)/shard_map/ppermute | solution.py:128
  257.1 32.1 %collective-permute-start.30 = (bf16[16,48,1536]{2,1,0:T(8,128)(2,1)}, bf16[16,48,1536]{2,1,0:T(8,128)(2,1)}, u32[]{:S(2)}, u32[]{:S(2)}) collective-permute-start(bf16[16,48,1536]{2,1,0:T(8,128)(2,1)} %get-tuple-element.66), channel_id=1, source_target_pairs={{0,16},{1,17},{2,18},{3,19},{4,20},{5,21},{6,22},{7,23},{8,24},{9,... | collective-permute-start | bytes 7077896 | tf_op jit(solution)/shard_map/ppermute | solution.py:128
  276.9 22.1 %collective-permute-start.36 = (bf16[16,96,768]{2,1,0:T(8,128)(2,1)}, bf16[16,96,768]{2,1,0:T(8,128)(2,1)}, u32[]{:S(2)}, u32[]{:S(2)}) collective-permute-start(bf16[16,96,768]{2,1,0:T(8,128)(2,1)} %get-tuple-element.68), channel_id=1, source_target_pairs={{0,16},{1,17},{2,18},{3,19},{4,20},{5,21},{6,22},{7,23},{8,24},{9,... | collective-permute-start | bytes 7077896 | tf_op jit(solution)/shard_map/ppermute | solution.py:128
  281.8 14.4 %collective-permute-start.19 = (bf16[8,48,1280]{2,1,0:T(8,128)(2,1)}, bf16[8,48,1280]{2,1,0:T(8,128)(2,1)}, u32[]{:S(2)}, u32[]{:S(2)}) collective-permute-start(bf16[8,48,1280]{2,1,0:T(8,128)(2,1)} %get-tuple-element.79), channel_id=1, source_target_pairs={{0,1},{1,0},{2,3},{3,2},{4,5},{5,4},{6,7},{7,6},{8,9},{9,8},{10,11... | collective-permute-start | bytes 2949128 | tf_op jit(solution)/shard_map/ppermute | solution.py:128
  291.6 22.4 %collective-permute-start.31 = (bf16[8,48,1536]{2,1,0:T(8,128)(2,1)S(1)}, bf16[8,48,1536]{2,1,0:T(8,128)(2,1)S(1)}, u32[]{:S(2)}, u32[]{:S(2)}) collective-permute-start(bf16[8,48,1536]{2,1,0:T(8,128)(2,1)S(1)} %get-tuple-element.77), channel_id=1, source_target_pairs={{0,1},{1,0},{2,3},{3,2},{4,5},{5,4},{6,7},{7,6},{8,9},{9,8},{10,11... | collective-permute-start | bytes 3538952 | tf_op jit(solution)/shard_map/ppermute | solution.py:128
  297.8 14.2 %collective-permute-start.20 = (bf16[4,48,1280]{2,1,0:T(8,128)(2,1)S(1)}, bf16[4,48,1280]{2,1,0:T(8,128)(2,1)S(1)}, u32[]{:S(2)}, u32[]{:S(2)}) collective-permute-start(bf16[4,48,1280]{2,1,0:T(8,128)(2,1)S(1)} %get-tuple-element.85), channel_id=1, source_target_pairs={{0,2},{1,3},{2,0},{3,1},{4,6},{5,7},{6,4},{7,5},{8,10},{9,11},{10,... | collective-permute-start | bytes 1474568 | tf_op jit(solution)/shard_map/ppermute | solution.py:128
  301.4 31.6 %collective-permute-start.37 = (bf16[8,96,768]{2,1,0:T(8,128)(2,1)S(1)}, bf16[8,96,768]{2,1,0:T(8,128)(2,1)S(1)}, u32[]{:S(2)}, u32[]{:S(2)}) collective-permute-start(bf16[8,96,768]{2,1,0:T(8,128)(2,1)S(1)} %get-tuple-element.75), channel_id=1, source_target_pairs={{0,1},{1,0},{2,3},{3,2},{4,5},{5,4},{6,7},{7,6},{8,9},{9,8},{10,11... | collective-permute-start | bytes 3538952 | tf_op jit(solution)/shard_map/ppermute | solution.py:128
  314.3 23.1 %collective-permute-start.32 = (bf16[4,48,1536]{2,1,0:T(8,128)(2,1)S(1)}, bf16[4,48,1536]{2,1,0:T(8,128)(2,1)S(1)}, u32[]{:S(2)}, u32[]{:S(2)}) collective-permute-start(bf16[4,48,1536]{2,1,0:T(8,128)(2,1)S(1)} %get-tuple-element.83), channel_id=1, source_target_pairs={{0,2},{1,3},{2,0},{3,1},{4,6},{5,7},{6,4},{7,5},{8,10},{9,11},{10,... | collective-permute-start | bytes 1769480 | tf_op jit(solution)/shard_map/ppermute | solution.py:128
  318.6 16.0 %collective-permute-start.22 = (bf16[1,48,1280]{2,1,0:T(8,128)(2,1)S(1)}, bf16[1,48,1280]{2,1,0:T(8,128)(2,1)S(1)}, u32[]{:S(2)}, u32[]{:S(2)}) collective-permute-start(bf16[1,48,1280]{2,1,0:T(8,128)(2,1)S(1)} %add_convert_fusion.24), channel_id=1, source_target_pairs={{0,8},{1,9},{2,10},{3,11},{4,12},{5,13},{6,14},{7,15},{8,0},{9,1},... | collective-permute-start | bytes 368648 | tf_op jit(solution)/shard_map/ppermute | solution.py:128
  (37 other events, 371.1 us)

commit v2 on v1

v2 whole, which is shorter than its diff:
```python
import functools

import jax
import jax.numpy as jnp
import numpy as np
from jax import lax
from jax.experimental import pallas as pl
from jax.experimental.pallas import tpu as pltpu
from jax.sharding import PartitionSpec as P

H = 12
DK = 64
BUCKETS = 32
BLOCK = 512
norm_eps = 1e-06
bucket_edges = (12, 16, 23, 32, 46, 64, 91)
MASKED = -1e30
F32 = jnp.float32
BF16 = jnp.bfloat16
PAIR = 2 * BLOCK
GROUPS = ((0, 512), (512, 256), (768, 128), (896, 128))
SPAN = 1024
SCOPED = {
    "qkv": 7,
    "attend": 5,
    "mid": 8,
    "outer_grad": 4,
    "out": 10,
    "mid_back": 10,
    "mid_grad": 3,
    "attend_back": 9,
    "qkv_grad": 3,
    "in_back": 13,
}


def bucket_of(relative):
    distance = jnp.abs(relative)
    passed = sum(((distance >= edge_value).astype(jnp.int32) for edge_value in bucket_edges))
    return jnp.where(relative > 0, BUCKETS // 2, 0) + jnp.where(
        distance < BUCKETS // 4, distance, BUCKETS // 4 + passed
    )


class Ring:
    def __init__(self, mesh, split=False):
        self.n = mesh.shape["fsdp"]
        self.bits = self.n.bit_length() - 1
        high = list(range(self.bits - 1, 1, -1))
        if split:
            self.order = ([0] + high + [1], [1] + high + [0])
        else:
            self.order = (high + [1, 0], high + [0, 1])

    def swap_phase(self, k):
        n = self.n
        return [
            (c * n + f, c * n + (f ^ (1 << self.order[c][k])))
            for c in range(2)
            for f in range(n)
        ]

    def swap_core(self):
        n = self.n
        return [(c * n + f, (1 - c) * n + f) for c in range(2) for f in range(n)]

    def meta(self):
        me = lax.axis_index("fsdp").astype(jnp.int32)
        core = lax.axis_index("dp").astype(jnp.int32)
        spots = jnp.arange(self.n, dtype=jnp.int32)

        def off(which):
            out = jnp.zeros_like(spots)
            for k, b in enumerate(self.order[which]):
                out = out | (((spots >> k) & 1) << b)
            return out

        def inv(which, m):
            out = jnp.zeros_like(spots)
            for k, b in enumerate(self.order[which]):
                out = out | (((m >> b) & 1) << k)
            return out

        first = core == 0
        mixed = me ^ spots
        return jnp.concatenate(
            [
                core[None],
                me ^ jnp.where(first, off(0), off(1)),
                me ^ jnp.where(first, off(1), off(0)),
                jnp.where(first, inv(0, mixed), inv(1, mixed)),
                jnp.where(first, inv(1, mixed), inv(0, mixed)),
            ]
        )


    def flip_origin(self, pieces):
        me = lax.axis_index("fsdp")
        shape = pieces.shape
        pieces = pieces.reshape((2,) * self.bits + shape[1:])
        for b in range(self.bits):
            axis = self.bits - 1 - b
            pieces = jnp.where((me >> b) & 1 == 1, jnp.flip(pieces, axis), pieces)
        return pieces.reshape(shape)

    def reorder(self, pieces, first, back):
        shape = pieces.shape
        split = pieces.reshape((2,) * self.bits + shape[1:])
        tail = list(range(self.bits, self.bits + len(shape) - 1))
        found = []
        for order in self.order:
            axes = [self.bits - 1 - order.index(self.bits - 1 - a) for a in range(self.bits)]
            if back:
                axes = list(np.argsort(axes))
            found.append(jnp.transpose(split, [int(a) for a in axes] + tail).reshape(shape))
        return jnp.where(first, found[0], found[1])

    def to_origin(self, pieces, first):
        return self.flip_origin(self.reorder(pieces, first, False))

    def from_origin(self, pieces, first):
        return self.reorder(self.flip_origin(pieces), first, True)


def shift(value, pairs):
    return lax.ppermute(value, ("dp", "fsdp"), pairs)


def after(value, *others):
    return lax.optimization_barrier((value, *others))[0]


class Gather:
    def __init__(self, ring, shard):
        self.ring = ring
        self.held = shard[None]
        self.phase = 0
        self.last = None
        self.got = None

    def join(self, *others):
        if self.got is not None:
            got = after(self.got, *others) if others else self.got
            self.held = jnp.concatenate([self.held, got], axis=0)
            self.got = None

    def go(self):
        got = shift(self.held, self.ring.swap_phase(self.phase))
        self.phase += 1
        if self.phase == self.ring.bits:
            self.last = got
        else:
            self.got = got
        return got

    def step(self, *others):
        self.join()
        if others:
            self.held = after(self.held, *others)
        got = self.go()
        return got

    def near(self):
        self.join()
        return self.held

    def finish(self, *others):
        own = (self.held, after(self.last, *others) if others else self.last)
        return own, tuple(shift(p, self.ring.swap_core()) for p in own)


def ready(*moves):
    for move, held in zip(moves, lax.optimization_barrier(tuple(m.held for m in moves))):
        move.held = held


def gather_on(values, *moves):
    values = tuple(values)
    flat = list(values)
    for move in moves:
        move.join(*values)
        flat.append(move.held)
        if move.last is not None:
            flat.append(move.last)
    flat = list(lax.optimization_barrier(tuple(flat)))
    values = [flat.pop(0) for _ in values]
    for move in moves:
        move.held = flat.pop(0)
        if move.last is not None:
            move.last = flat.pop(0)
        else:
            move.go()
    return values


def gather_pieces(ring, shard):
    move = Gather(ring, shard)
    for _ in range(ring.bits):
        move.step()
    return move.finish()


class Reduce:
    def __init__(self, ring, keep, send):
        self.ring = ring
        self.keep = keep
        self.away = send
        self.got = None
        self.phase = ring.bits + 1

    def step(self, *others):
        got = after(self.got, *others) if others else self.got
        self.got = None
        if self.phase == 0:
            return self.keep[0].astype(F32) + got[0].astype(F32)
        half = self.keep.shape[0] // 2

        def add(part):
            return self.keep[part].astype(F32) + got[part].astype(F32)

        self.away = add(slice(half, None)).astype(BF16)
        self.keep = add(slice(0, half))
        if self.phase > 1:
            self.keep = self.keep.astype(BF16)

    def go(self):
        self.phase -= 1
        if self.phase == self.ring.bits:
            pairs = self.ring.swap_core()
        else:
            pairs = self.ring.swap_phase(self.phase)
        self.got = shift(self.away, pairs)

    def finish(self):
        while self.phase > 0:
            if self.got is not None:
                self.step()
            self.go()
        return self.step()


def tick(values, steps=(), fresh=()):
    values = tuple(values)
    for red in steps:
        red.step(*values)
    reds = [*steps, *fresh]
    flat = list(values)
    for red in reds:
        flat += [red.keep, red.away]
    flat = lax.optimization_barrier(tuple(flat))
    for i, red in enumerate(reds):
        red.keep, red.away = flat[len(values) + 2 * i : len(values) + 2 * i + 2]
        red.go()
    return flat[: len(values)]


def sum_all(ring, value):
    value = value + shift(value, ring.swap_core())
    for k in range(ring.bits):
        value = value + shift(value, ring.swap_phase(k))
    return value


def any_spec():
    return pl.BlockSpec(memory_space=pl.ANY)


def params(vmem):
    return pltpu.CompilerParams(vmem_limit_bytes=vmem)


def cost(flops, bytes_accessed, trans=0):
    return pl.CostEstimate(flops=flops, bytes_accessed=bytes_accessed, transcendentals=trans)


def dot(a, b):
    return jnp.dot(a, b, preferred_element_type=F32)


def dot_nt(a, b):
    return lax.dot_general(a, b, (((1,), (1,)), ((), ())), preferred_element_type=F32)


def dot_tn(a, b):
    return lax.dot_general(a, b, (((0,), (0,)), ((), ())), preferred_element_type=F32)


class Pieces:
    def __init__(self, own, rec, n, placed=False):
        self.arrays = [*own, *rec]
        self.n = n
        self.count = len(self.arrays)
        self.part = n // len(own)
        self.whole = False
        self.placed = placed

    def spot(self, meta, h, j):
        place = j if self.placed else meta[1 + h * self.n + j]
        return place, h * (self.count // 2) + j // self.part, j % self.part


class Whole:
    def __init__(self, array):
        self.arrays = [array]
        self.count = 1
        self.whole = True
        self.n = 0


def column_copies(chunk, meta, refs, lo, width, dst, sems, base=0, own_first=False):
    copies = []
    if chunk.whole:
        for h in range(2):
            side = (meta[0] if h == 0 else 1 - meta[0]) if own_first else h
            src = refs[0].at[side, :, pl.ds(lo, width)]
            copies.append(
                pltpu.make_async_copy(src, dst.at[:, pl.ds(h * width, width)], sems.at[base + h])
            )
        return copies
    n = chunk.n
    rows = refs[0].shape[1]
    core = meta[0]
    for h in range(2):
        side = h if own_first else (core if h == 0 else 1 - core)
        col = pl.multiple_of(side * width, 128)
        for j in range(n):
            place, which, index = chunk.spot(meta, h, j)
            row = pl.multiple_of(place * rows, 16)
            copies.append(
                pltpu.make_async_copy(
                    refs[which].at[index, :, pl.ds(lo, width)],
                    dst.at[pl.ds(row, rows), pl.ds(col, width)],
                    sems.at[base + h * n + j],
                )
            )
    return copies


def row_copies(chunk, meta, refs, dst, sems, base=0):
    if chunk.whole:
        return [pltpu.make_async_copy(refs[0], dst, sems.at[base])]
    n = chunk.n
    rows = refs[0].shape[1]
    core = meta[0]
    copies = []
    for h in range(2):
        for j in range(n):
            place, which, index = chunk.spot(meta, h, j)
            row = pl.multiple_of(
                place * (2 * rows) + (core if h == 0 else 1 - core) * rows, 16
            )
            copies.append(
                pltpu.make_async_copy(
                    refs[which].at[index], dst.at[pl.ds(row, rows), :], sems.at[base + h * n + j]
                )
            )
    return copies


def run_copies(copies):
    for c in copies:
        c.start()
    for c in copies:
        c.wait()


def copy_count(chunk):
    return 2 if chunk.whole else 2 * chunk.n


def norm_tile(x, ext_ref, first):
    d = x.shape[1]
    scale = lax.rsqrt(jnp.mean(x * x, axis=-1, keepdims=True) + norm_eps)
    out = []
    for c in range(d // 128):
        out.append(
            (x[:, c * 128 : (c + 1) * 128] * scale * ext_ref[first + c : first + c + 1, :]).astype(
                BF16
            )
        )
    return jnp.concatenate(out, axis=1), scale


def call(body, name, inputs, anys, outs, scratch, flops, trans=0, aliases=None):
    meta, *arrays = inputs
    moved = sum(a.size * a.dtype.itemsize for a in [*arrays, *anys])
    moved += sum(int(np.prod(o.shape)) * jnp.dtype(o.dtype).itemsize for o in outs)
    vmem_spec = pl.BlockSpec(memory_space=pltpu.VMEM)
    return pl.pallas_call(
        body,
        in_specs=[pl.BlockSpec(memory_space=pltpu.SMEM)]
        + [vmem_spec] * len(arrays)
        + [any_spec()] * len(anys),
        out_specs=[vmem_spec] * len(outs),
        out_shape=outs,
        scratch_shapes=scratch,
        input_output_aliases=aliases or {},
        compiler_params=params(SCOPED[name] * 1024 * 1024),
        cost_estimate=cost(flops, moved, trans),
        name=name,
    )(meta, *arrays, *anys)


def array(shape, dtype):
    return jax.ShapeDtypeStruct(shape, dtype)


def qkv_kernel(chunk, tile, meta, x_ref, ext_ref, *rest):
    refs = rest[: chunk.count]
    qkv_ref, n_ref, dist_ref, w, sems = rest[chunk.count :]
    copies = column_copies(chunk, meta, refs, 0, w.shape[1] // 2, w, sems)
    for c in copies:
        c.start()
    place = lax.broadcasted_iota(jnp.int32, (BUCKETS, SPAN), 1)
    row = lax.broadcasted_iota(jnp.int32, (BUCKETS, SPAN), 0)
    chosen = (bucket_of(BLOCK - 1 - place) == row).astype(F32).astype(BF16)
    dist_ref[...] = dot(ext_ref[16:32, 0:BUCKETS].astype(BF16), chosen)
    rows = x_ref.shape[0]
    for r in range(0, rows, tile):
        n_ref[r : r + tile, :] = norm_tile(x_ref[r : r + tile, :].astype(F32), ext_ref, 0)[0]
    for c in copies:
        c.wait()
    for c in range(0, w.shape[1], 256):
        qkv_ref[:, c : c + 256] = dot(n_ref[...], w[:, c : c + 256]).astype(BF16)


def qkv_call(meta, x, ext, chunk):
    rows, d = x.shape
    return call(
        functools.partial(qkv_kernel, chunk, rows // 4),
        "qkv",
        (meta, x, ext),
        chunk.arrays,
        [array((rows, 3 * d), BF16), array((rows, d), BF16), array((16, SPAN), F32)],
        [pltpu.VMEM((d, 3 * d), BF16), pltpu.SemaphoreType.DMA((copy_count(chunk),))],
        6 * rows * d * d,
    )


def bias_strip(dist_row):
    spread = jnp.broadcast_to(dist_row, (128, SPAN))
    return pltpu.roll(spread, SPAN - 127, 1, stride=1, stride_axis=0)


def strip_bias(strip, size, i0, step):
    return jnp.concatenate(
        [
            strip[:, (3 - t) * 128 + i0 : (3 - t) * 128 + i0 + step]
            for t in range(size // 128)
        ],
        axis=0,
    )


def attend_kernel(first, count, meta, qkv_ref, qaug_ref, kaug_ref, dist_ref, ctx_ref, lse_ref):
    rows = qkv_ref.shape[0]
    for base in range(0, rows, PAIR):
        lane = lax.broadcasted_iota(jnp.int32, (PAIR, 128), 1)
        qaug, kaug = qaug_ref[base : base + PAIR, :], kaug_ref[base : base + PAIR, :]
        for pair in range(count):
            at = first + pair
            col = (at // 3) * 9 * 128 + (at % 3) * 128
            q = qkv_ref[base : base + PAIR, col : col + 128]
            k = qkv_ref[base : base + PAIR, col + 384 : col + 512]
            v_turned = qkv_ref[base : base + PAIR, col + 768 : col + 896].T
            heads = []
            for hh in range(2):
                mine = (lane // 64) == hh
                heads.append(
                    (
                        jnp.where(mine, q, qaug),
                        jnp.where(mine, k, kaug),
                        v_turned[hh * 64 : (hh + 1) * 64, :],
                        bias_strip(dist_ref[2 * at + hh : 2 * at + hh + 1, :]),
                    )
                )
            for off, size in GROUPS:
                step = min(256, size)
                for i0 in range(0, size, step):
                    lo, hi = off + i0, off + i0 + step
                    parts = []
                    for hh in range(2):
                        qa, ka, vt, strip = heads[hh]
                        scores = dot_nt(ka[off : off + size], qa[lo:hi])
                        scores = scores + strip_bias(strip, size, i0, step)
                        top = jnp.max(scores, axis=0, keepdims=True)
                        expo = jnp.exp(scores - top)
                        total = jnp.sum(expo, axis=0, keepdims=True)
                        mixed = dot(vt[:, off : off + size], expo.astype(BF16))
                        parts.append(mixed * (1.0 / total))
                        lse_ref[2 * pair + hh : 2 * pair + hh + 1, base + lo : base + hi] = (
                            top + jnp.log(total)
                        )
                    both = jnp.concatenate(parts, axis=0)
                    ctx_ref[base + lo : base + hi, pair * 128 : (pair + 1) * 128] = both.T.astype(
                        BF16
                    )


def attend_call(meta, qkv, qaug, kaug, dist, first, count):
    rows = qkv.shape[0]
    pairs = rows // PAIR
    return call(
        functools.partial(attend_kernel, first, count),
        "attend",
        (meta, qkv, qaug, kaug, dist),
        (),
        [array((rows, count * 128), BF16), array((2 * count, rows), F32)],
        [],
        8 * pairs * count * 350000 * 128,
        trans=2 * pairs * count * 350000,
    )


def mid_kernel(chunk, tile, meta, low_ref, high_ref, x_ref, ext_ref, *rest):
    refs = rest[: chunk.count]
    mid_ref, n2_ref, act_ref, slope_ref, wo, w1, sems = rest[chunk.count :]
    d = wo.shape[0]
    n = copy_count(chunk)
    first = column_copies(chunk, meta, refs, 0, d // 2, wo, sems)
    second = column_copies(chunk, meta, refs, d // 2, w1.shape[1] // 2, w1, sems, n)
    for c in first + second:
        c.start()
    for c in first:
        c.wait()
    rows = x_ref.shape[0]
    for r in range(0, rows, tile):
        span = slice(r, r + tile)
        ctx = jnp.concatenate([low_ref[span, :], high_ref[span, :]], axis=1)
        middle = x_ref[span, :].astype(F32) + dot(ctx, wo[...])
        mid_ref[span, :] = middle
        n2_ref[span, :] = norm_tile(middle, ext_ref, 6)[0]
    for c in second:
        c.wait()
    c0 = 0.7978845608028654
    c1 = c0 * 0.044715
    step = 256
    for f in range(0, w1.shape[1], step):
        for r in range(0, rows, tile):
            span = slice(r, r + tile)
            v = dot(n2_ref[span, :], w1[:, f : f + step])
            v2 = v * v
            half = 0.5 + 0.5 * jnp.tanh(v * (c0 + c1 * v2))
            active = v * half
            act_ref[span, f : f + step] = active.astype(BF16)
            slope_ref[span, f : f + step] = (
                half + (active - active * half) * (2.0 * c0 + (6.0 * c1) * v2)
            ).astype(BF16)


def mid_call(meta, ctxs, x, ext, chunk, ff):
    rows, d = x.shape
    return call(
        functools.partial(mid_kernel, chunk, rows // 4),
        "mid",
        (meta, *ctxs, x, ext),
        chunk.arrays,
        [
            array((rows, d), F32),
            array((rows, d), BF16),
            array((rows, ff), BF16),
            array((rows, ff), BF16),
        ],
        [
            pltpu.VMEM((d, d), BF16),
            pltpu.VMEM((d, ff), BF16),
            pltpu.SemaphoreType.DMA((2 * copy_count(chunk),)),
        ],
        2 * rows * d * (d + ff),
        trans=rows * ff,
    )


def outer_grad_kernel(n, meta, act_ref, g_ref, keep_ref, send_ref):
    per = keep_ref.shape[1]
    first = meta[0] == 0
    width = 4 * per * 2
    for b in range(act_ref.shape[1] // width):
        total = dot_tn(act_ref[:, b * width : (b + 1) * width], g_ref[...]).astype(BF16)
        for f in range(4):
            low = total[2 * f * per : (2 * f + 1) * per]
            high = total[(2 * f + 1) * per : (2 * f + 2) * per]
            spot = b * 4 + f
            keep_ref[meta[1 + 2 * n + spot]] = jnp.where(first, low, high)
            send_ref[meta[1 + 3 * n + spot]] = jnp.where(first, high, low)


def outer_grad_call(meta, act, g, n):
    rows, ff = act.shape
    d = g.shape[1]
    shape = array((n, ff // n // 2, d), BF16)
    return call(
        functools.partial(outer_grad_kernel, n),
        "outer_grad",
        (meta, act, g),
        (),
        [shape, shape],
        [],
        2 * rows * d * ff,
    )


def out_kernel(chunk, tile, meta, act_ref, mid_ref, g_ref, slope_ref, *rest):
    refs = rest[: chunk.count]
    result_ref, din_ref, w2, sems = rest[chunk.count :]
    run_copies(row_copies(chunk, meta, refs, w2, sems))
    rows = g_ref.shape[0]
    step = 256
    for f in range(0, w2.shape[0], step):
        for r in range(0, rows, tile):
            span = slice(r, r + tile)
            d_act = dot_nt(g_ref[span, :], w2[f : f + step, :])
            slope = slope_ref[span, f : f + step].astype(F32)
            din_ref[span, f : f + step] = (d_act * slope).astype(BF16)
    for c in range(0, w2.shape[1], step):
        result_ref[:, c : c + step] = mid_ref[:, c : c + step] + dot(
            act_ref[...], w2[:, c : c + step]
        )


def out_call(meta, act, middle, g, slope, chunk):
    rows, ff = act.shape
    d = middle.shape[1]
    return call(
        functools.partial(out_kernel, chunk, rows // 4),
        "out",
        (meta, act, middle, g, slope),
        chunk.arrays,
        [array((rows, d), F32), array((rows, ff), BF16)],
        [pltpu.VMEM((ff, d), BF16), pltpu.SemaphoreType.DMA((copy_count(chunk),))],
        4 * rows * d * ff,
        aliases={4: 1},
    )


def store_pieces(out, spots, base, total, rows, cols, first=0):
    for f in range(total.shape[0] // rows):
        out[spots[base + first + f], :, cols] = total[f * rows : (f + 1) * rows]


def mid_grad_kernel(n, meta, n2_ref, low_ref, high_ref, din_ref, datt_ref, keep_ref, send_ref):
    per = keep_ref.shape[1]
    h = datt_ref.shape[1] // 2
    ffh = din_ref.shape[1] // 2
    step = 512
    for out, side, table in ((send_ref, 1 - meta[0], 3), (keep_ref, meta[0], 2)):
        base = 1 + table * n
        col = pl.multiple_of(side * h, 128)
        datt = datt_ref[:, pl.ds(col, h)]
        for part, c_ref in enumerate((low_ref, high_ref)):
            total = dot_tn(c_ref[...], datt).astype(BF16)
            store_pieces(out, meta, base, total, per, slice(0, h), part * (n // 2))
        for c in range(0, ffh, step):
            col = pl.multiple_of(side * ffh + c, 128)
            total = dot_tn(n2_ref[...], din_ref[:, pl.ds(col, step)]).astype(BF16)
            store_pieces(out, meta, base, total, per, slice(h + c, h + c + step))


def mid_grad_call(meta, n2, ctxs, d_inner, d_att, n):
    rows, d = n2.shape
    ff = d_inner.shape[1]
    shape = array((n, d // n, (d + ff) // 2), BF16)
    return call(
        functools.partial(mid_grad_kernel, n),
        "mid_grad",
        (meta, n2, *ctxs, d_inner, d_att),
        (),
        [shape, shape],
        [],
        2 * rows * d * (d + ff),
    )


def qkv_grad_kernel(n, table, meta, n_ref, d_ref, out_ref):
    h = d_ref.shape[2]
    for t in range(3):
        total = dot_tn(n_ref[...], d_ref[t]).astype(BF16)
        store_pieces(
            out_ref, meta, 1 + table * n, total, out_ref.shape[1], slice(t * h, (t + 1) * h)
        )


def qkv_grad_call(meta, normed, dqkv, n, table):
    rows, d = normed.shape
    h = dqkv.shape[2]
    return call(
        functools.partial(qkv_grad_kernel, n, table),
        "qkv_grad",
        (meta, normed, dqkv),
        (),
        [array((n, d // n, 3 * h), BF16)],
        [],
        6 * rows * d * h,
    )[0]


def norm_back(dn, x, gain_ref, first, scale):
    d = x.shape[1]
    z = jnp.concatenate(
        [
            dn[:, c * 128 : (c + 1) * 128] * gain_ref[first + c : first + c + 1, :]
            for c in range(d // 128)
        ],
        axis=1,
    )
    inner = jnp.mean(z * x, axis=-1, keepdims=True)
    back = scale * z - x * (scale * scale * scale * inner)
    return back, jnp.sum(dn * (x * scale), axis=0, keepdims=True)


def mid_back_kernel(chunk, tile, meta, din_ref, mid_ref, g_ref, ext_ref, *rest):
    refs = rest[: chunk.count]
    dmid_ref, datt_ref, dctx_ref, gain_ref, wo, w1, sems = rest[chunk.count :]
    d = wo.shape[0]
    n = copy_count(chunk)
    first = column_copies(chunk, meta, refs, d // 2, w1.shape[1] // 2, w1, sems, n)
    second = column_copies(chunk, meta, refs, 0, d // 2, wo, sems)
    for c in first + second:
        c.start()
    for c in first:
        c.wait()
    rows = g_ref.shape[0]
    gains = []
    for r in range(0, rows, tile):
        span = slice(r, r + tile)
        dn = dot_nt(din_ref[span, :], w1[...])
        middle = mid_ref[span, :]
        scale = lax.rsqrt(jnp.mean(middle * middle, axis=-1, keepdims=True) + norm_eps)
        back, gain = norm_back(dn, middle, ext_ref, 6, scale)
        gains.append(gain)
        dmid = g_ref[span, :].astype(F32) + back
        dmid_ref[span, :] = dmid
        datt_ref[span, :] = dmid.astype(BF16)
        if r == 0:
            for c in second:
                c.wait()
        dctx_ref[span, :] = dot_nt(datt_ref[span, :], wo[...]).astype(BF16)
    gain_ref[...] = sum(gains)


def mid_back_call(meta, din, middle, g, ext, chunk):
    rows, ff = din.shape
    d = middle.shape[1]
    return call(
        functools.partial(mid_back_kernel, chunk, rows // 4),
        "mid_back",
        (meta, din, middle, g, ext),
        chunk.arrays,
        [
            array((rows, d), F32),
            array((rows, d), BF16),
            array((rows, d), BF16),
            array((1, d), F32),
        ],
        [
            pltpu.VMEM((d, d), BF16),
            pltpu.VMEM((d, ff), BF16),
            pltpu.SemaphoreType.DMA((2 * copy_count(chunk),)),
        ],
        2 * rows * d * (d + ff),
    )


def diagonal_sums(strip):
    for s in (64, 32, 16, 8):
        strip = strip[:s] + pltpu.roll(strip[s:], SPAN - s, 1)
    for s in (4, 2, 1):
        strip = strip + pltpu.roll(pltpu.roll(strip, 8 - s, 0), SPAN - s, 1)
    return strip[:1]


def attend_back_kernel(
    keep,
    meta,
    qkv_ref,
    dctx_ref,
    qaug_ref,
    kaug_ref,
    dist_ref,
    lse_ref,
    grad_ref,
    table_ref,
    strip_acc,
):
    side = meta[0] if keep else 1 - meta[0]
    count = H // 4
    rows = qkv_ref.shape[0]
    lane = lax.broadcasted_iota(jnp.int32, (PAIR, 128), 1)
    for pair in range(count):
        strip_acc[...] = jnp.zeros_like(strip_acc)
        strips = [
            bias_strip(dist_ref[pl.ds(side * 6 + 2 * pair + hh, 1), :]) for hh in range(2)
        ]
        for base in range(0, rows, PAIR):
            block = slice(base, base + PAIR)

            def part(t):
                col = pl.multiple_of(side * 1152 + (t * 3 + pair) * 128, 128)
                return qkv_ref[block, pl.ds(col, 128)]

            q, k, v = part(0), part(1), part(2)
            do = dctx_ref[block, pl.ds(pl.multiple_of(side * 384 + pair * 128, 128), 128)]
            lse = [lse_ref[pl.ds(side * 6 + 2 * pair + hh, 1), block] for hh in range(2)]
            qaug, kaug = qaug_ref[block, :], kaug_ref[block, :]
            k_turned = k.T
            heads = []
            for hh in range(2):
                mine = (lane // 64) == hh
                heads.append(
                    (
                        jnp.where(mine, q, qaug),
                        jnp.where(mine, k, kaug),
                        jnp.where(mine, v, jnp.zeros_like(v)),
                        k_turned[hh * 64 : (hh + 1) * 64, :],
                        strips[hh],
                    )
                )
            cols = slice(pair * 128, (pair + 1) * 128)
            for off, size in GROUPS:
                step = min(256, size)
                low = lax.broadcasted_iota(jnp.int32, (size, 128), 1) < 64
                dks, dvs = [None, None], [None, None]
                for i0 in range(0, size, step):
                    lo, hi = off + i0, off + i0 + step
                    dqs = []
                    for hh in range(2):
                        qa, ka, va, kt, strip = heads[hh]
                        scores = dot_nt(ka[off : off + size], qa[lo:hi])
                        scores = scores + strip_bias(strip, size, i0, step)
                        probs = jnp.exp(scores - lse[hh][:, lo:hi])
                        d_probs = dot_nt(va[off : off + size], do[lo:hi])
                        dv = dot(probs.astype(BF16), do[lo:hi])
                        center = jnp.sum(probs * d_probs, axis=0, keepdims=True)
                        d_scores = probs * (d_probs - center)
                        for t in range(size // 128):
                            at = (3 - t) * 128 + i0
                            strip_acc[hh, :, at : at + step] += d_scores[t * 128 : (t + 1) * 128]
                        ds_low = d_scores.astype(BF16)
                        dk = dot(ds_low, q[lo:hi])
                        dqs.append(dot(kt[:, off : off + size], ds_low))
                        dks[hh] = dk if dks[hh] is None else dks[hh] + dk
                        dvs[hh] = dv if dvs[hh] is None else dvs[hh] + dv
                    dq = jnp.concatenate(dqs, axis=0).T.astype(BF16)
                    grad_ref[0, base + lo : base + hi, cols] = dq
                out = slice(base + off, base + off + size)
                grad_ref[1, out, cols] = jnp.where(low, dks[0], dks[1]).astype(BF16)
                grad_ref[2, out, cols] = jnp.where(low, dvs[0], dvs[1]).astype(BF16)
        for hh in range(2):
            table_ref[2 * pair + hh : 2 * pair + hh + 1, :] = diagonal_sums(strip_acc[hh])
    table_ref[2 * count :, :] = jnp.zeros((8 - 2 * count, SPAN), F32)


def attend_back_call(meta, qkv, dctx, qaug, kaug, dist, lse, keep):
    rows, d = dctx.shape
    pairs = rows // PAIR
    count = H // 4
    return call(
        functools.partial(attend_back_kernel, keep),
        "attend_back",
        (meta, qkv, dctx, qaug, kaug, dist, lse),
        (),
        [array((3, rows, count * 128), BF16), array((8, SPAN), F32)],
        [pltpu.VMEM((2, 128, SPAN), F32)],
        20 * pairs * count * 350000 * 128,
        trans=2 * pairs * count * 350000,
    )


def in_back_kernel(chunk, tile, meta, own_ref, rec_ref, x_ref, dmid_ref, ext_ref, *rest):
    stay_ref, away_ref, gain_ref, *rest = rest
    refs = rest[: chunk.count]
    dx_ref, extra_ref, w, sems = rest[chunk.count :]
    copies = column_copies(chunk, meta, refs, 0, w.shape[1] // 2, w, sems, own_first=True)
    for c in copies:
        c.start()
    place = (lax.broadcasted_iota(jnp.int32, (128, SPAN), 1) + 127) % SPAN
    row = lax.broadcasted_iota(jnp.int32, (128, SPAN), 0)
    chosen = (bucket_of(BLOCK - 1 - place) == row).astype(F32)
    found = [
        lax.dot_general(
            r[...],
            chosen,
            (((1,), (1,)), ((), ())),
            precision=lax.Precision.HIGHEST,
            preferred_element_type=F32,
        )[: H // 2]
        for r in (stay_ref, away_ref)
    ]
    first = meta[0] == 0
    extra_ref[...] = jnp.zeros_like(extra_ref)
    extra_ref[16 : 16 + H // 2, :] = jnp.where(first, found[0], found[1])
    extra_ref[16 + H // 2 : 16 + H, :] = jnp.where(first, found[1], found[0])
    for c in copies:
        c.wait()
    rows, d = x_ref.shape
    gains = []
    for r in range(0, rows, tile):
        span = slice(r, r + tile)
        parts = [ref[t, span, :] for ref in (own_ref, rec_ref) for t in range(3)]
        dn = dot_nt(jnp.concatenate(parts, axis=1), w[...])
        x = x_ref[span, :].astype(F32)
        scale = lax.rsqrt(jnp.mean(x * x, axis=-1, keepdims=True) + norm_eps)
        back, gain = norm_back(dn, x, ext_ref, 0, scale)
        gains.append(gain)
        dx_ref[span, :] = dmid_ref[span, :] + back
    total = sum(gains)
    for c in range(d // 128):
        extra_ref[c : c + 1, :] = total[:, c * 128 : (c + 1) * 128]
        extra_ref[6 + c : 7 + c, :] = gain_ref[:, c * 128 : (c + 1) * 128]


def in_back_call(meta, own, rec, x, dmid, ext, found, gain, chunk):
    rows, d = x.shape
    return call(
        functools.partial(in_back_kernel, chunk, rows // 4),
        "in_back",
        (meta, own, rec, x, dmid, ext, *found, gain),
        chunk.arrays,
        [array((rows, d), F32), array((32, 128), F32)],
        [pltpu.VMEM((d, 3 * d), BF16), pltpu.SemaphoreType.DMA((copy_count(chunk),))],
        6 * rows * d * d,
    )


def mask_lanes(lengths, rows):
    spot = jnp.arange(rows, dtype=jnp.int32)
    within = spot % PAIR
    first = jnp.array([0, 512, 768, 896, 960], jnp.int32)
    slot = jnp.sum((within[:, None] >= first[None, 1:]).astype(jnp.int32), axis=1)
    start = jnp.sum(jnp.where(slot[:, None] == jnp.arange(5)[None], first[None], 0), axis=1)
    docs = jnp.arange(lengths.shape[0], dtype=jnp.int32)
    document = spot // PAIR * 5 + slot
    own = jnp.sum(jnp.where(document[:, None] == docs[None], lengths[None], 0), axis=1)
    live = within - start < own
    late = slot == 4
    lane = jnp.arange(128, dtype=jnp.int32) % 64
    shown = [live & ~late, live & late]
    kaug = jnp.where(
        lane[None] == 0,
        jnp.where(shown[0], 0.0, MASKED)[:, None],
        jnp.where(lane[None] == 1, jnp.where(shown[1], 0.0, MASKED)[:, None], 0.0),
    ).astype(BF16)
    qaug = jnp.where(
        lane[None] == 0,
        jnp.where(late, 0.0, 1.0)[:, None],
        jnp.where(lane[None] == 1, jnp.where(late, 1.0, 0.0)[:, None], 0.0),
    ).astype(BF16)
    return qaug, kaug, live


def placed_rows(vector, me, rows):
    count = vector.shape[0]
    spot = jnp.arange(rows * 128, dtype=jnp.int32)[None] - me * count
    hit = spot == jnp.arange(count, dtype=jnp.int32)[:, None]
    flat = jnp.sum(jnp.where(hit, vector.astype(F32)[:, None], 0.0), axis=0)
    return flat.reshape(rows, 128)


def placed_table(vector, me):
    count = vector.shape[0]
    head = jnp.arange(16, dtype=jnp.int32)[:, None]
    bucket = jnp.arange(128, dtype=jnp.int32)[None]
    entry = jnp.where((head < H) & (bucket < BUCKETS), bucket * H + head, -1) - me * count
    hit = entry[None] == jnp.arange(count, dtype=jnp.int32)[:, None, None]
    return jnp.sum(jnp.where(hit, vector.astype(F32)[:, None, None], 0.0), axis=0)


def local(
    ring,
    ring_c,
    hidden,
    gain_attn,
    rel_table,
    query_weight,
    key_weight,
    value_weight,
    output_weight,
    gain_ffn,
    inner_weight,
    outer_weight,
    lengths,
    cotangent,
):
    rows, d = hidden.shape
    ff = inner_weight.shape[1]
    n = ring.n
    shard_rows = query_weight.shape[0]
    outer_rows = outer_weight.shape[0]
    direct = shard_rows % 16 == 0 and shard_rows >= 32 and outer_rows % 32 == 0
    me = lax.axis_index("fsdp")
    core = lax.axis_index("dp")
    meta = ring.meta()
    meta_c = ring_c.meta()
    h = d // 2

    def half(w, which):
        width = w.shape[1] // 2
        return lax.dynamic_slice_in_dim(w, which * width, width, 1)

    small = jnp.concatenate(
        [
            placed_rows(gain_attn, me, d // 128),
            placed_rows(gain_ffn, me, d // 128),
            jnp.zeros((16 - 2 * (d // 128), 128), F32),
            placed_table(rel_table, me),
        ],
        axis=0,
    ).astype(BF16)
    pack_a = [half(w, core) for w in (query_weight, key_weight, value_weight)]
    if direct:
        pack_a.append(jnp.pad(small, ((0, shard_rows - 32), (0, 0))))
    pack_a = jnp.concatenate(pack_a, axis=1)
    pack_b = jnp.concatenate([half(output_weight, core), half(inner_weight, core)], axis=1)
    pack_c = lax.dynamic_slice_in_dim(
        outer_weight, core * (outer_rows // 2), outer_rows // 2, 0
    )

    def whole_columns(own, rec):
        both = []
        for parts, first in ((own, core == 0), (rec, core == 1)):
            pieces = ring.to_origin(jnp.concatenate(parts, axis=0), first)
            both.append(pieces.reshape(-1, pieces.shape[2]))
        first = jnp.where(core == 0, both[0], both[1])
        second = jnp.where(core == 0, both[1], both[0])
        return jnp.stack([first, second])

    qaug, kaug, live = mask_lanes(lengths, rows)
    g = jnp.where(live[:, None], cotangent, jnp.zeros_like(cotangent))
    if direct:
        move_a, move_b = Gather(ring, pack_a), Gather(ring, pack_b)
        move_c = Gather(ring_c, pack_c)
        move_a.go()
        move_c.go()
        for _ in range(ring.bits - 3):
            move_a.join(meta, meta_c, qaug, kaug, g)
            move_a.go()
        move_a.join()
        for _ in range(ring.bits - 3):
            ready(move_a, move_b)
            move_a.go()
            move_b.go()
            move_a.join()
            move_b.join()
        ready(move_a, move_b)
        move_a.go()
        move_b.go()
        move_a.last, move_b.got = lax.optimization_barrier((move_a.last, move_b.got))
        move_b.join()
        final = move_a.last
        move_b.held, final = lax.optimization_barrier((move_b.held, final))
        move_b.go()
        chunk_a = Pieces(*move_a.finish(), n)
        got_a = (chunk_a.arrays[:2],)
        move_c.join(final)
        move_c.go()
        ext = sum(jnp.sum(p[:, :32, 3 * h :].astype(F32), axis=0) for p in got_a[0])
    else:
        got_c = gather_pieces(ring, pack_c)
        chunk_a = Whole(whole_columns(*gather_pieces(ring, pack_a)))
        chunk_b = Whole(whole_columns(*gather_pieces(ring, pack_b)))
        both = [
            ring.to_origin(jnp.concatenate(parts, axis=0), first)
            for parts, first in zip(got_c, (core == 0, core == 1))
        ]
        first = jnp.where(core == 0, both[0], both[1])
        second = jnp.where(core == 0, both[1], both[0])
        chunk_c = Whole(jnp.stack([first, second], axis=1).reshape(ff, d))
        ext = lax.psum(small.astype(F32), "fsdp")

    qkv, normed, dist = qkv_call(meta, hidden, ext, chunk_a)
    if direct:
        (qkv,) = gather_on((qkv,), move_b, move_c)
    ctx0, lse0 = attend_call(meta, qkv, qaug, kaug, dist, 0, H // 4)
    if direct:
        dist, ctx0 = lax.optimization_barrier((dist, ctx0))
    ctx1, lse1 = attend_call(meta, qkv, qaug, kaug, dist, H // 4, H // 4)
    if direct:
        (ctx1,) = gather_on((ctx1,), move_b, move_c)
        chunk_b = Pieces(*move_b.finish(), n)
    ctxs = (ctx0, ctx1)
    middle, normed2, act, slope = mid_call(meta, ctxs, hidden, ext, chunk_b, ff)
    if direct:
        chunk_c = Pieces(*move_c.finish(act), n)

    def split_columns(pairs, which):
        full = [jnp.einsum("td,tf->df", a, b, preferred_element_type=F32) for a, b in pairs]
        part = jnp.concatenate(full, axis=1).astype(BF16)
        part = part.reshape(n, d // n, part.shape[1])
        return ring.from_origin(part, which == 0)

    if direct:
        grad_c = outer_grad_call(meta, act, g, n)
    else:
        full = jnp.einsum("tf,td->fd", act, g, preferred_element_type=F32).astype(BF16)
        full = full.reshape(n, 2, outer_rows // 2, d)
        grad_c = [
            ring.from_origin(
                lax.dynamic_index_in_dim(full, which, 1, keepdims=False), which == 0
            )
            for which in (core, 1 - core)
        ]
    red_c = Reduce(ring, *grad_c)
    (act,) = tick((act,), fresh=(red_c,))
    result, d_inner = out_call(meta_c, act, middle, g, slope, chunk_c)
    (d_inner,) = tick((d_inner,), (red_c,))
    d_middle, d_att, d_ctx, grad_gain_f = mid_back_call(meta, d_inner, middle, g, ext, chunk_b)
    (d_att,) = tick((d_att,), (red_c,))
    if direct:
        grad_b = mid_grad_call(meta, normed2, ctxs, d_inner, d_att, n)
    else:
        both = jnp.concatenate(ctxs, axis=1)
        grad_b = [
            split_columns([(both, half(d_att, w)), (normed2, half(d_inner, w))], w)
            for w in (core, 1 - core)
        ]
    red_b = Reduce(ring, *grad_b)
    (d_ctx,) = tick((after(d_ctx, *grad_b),), (red_c,), (red_b,))
    lse = jnp.concatenate([lse0, lse1], axis=0)
    away, found_away = attend_back_call(meta, qkv, d_ctx, qaug, kaug, dist, lse, False)
    (away,) = tick((away,), (red_c, red_b))
    if direct:
        send_a = qkv_grad_call(meta, normed, away, n, 3)
    else:
        send_a = split_columns([(normed, away[t]) for t in range(3)], 1 - core)
    d_ctx, send_a = lax.optimization_barrier((d_ctx, send_a))
    red_a = Reduce(ring, None, send_a)
    red_a.go()
    stay, found_stay = attend_back_call(meta, qkv, d_ctx, qaug, kaug, dist, lse, True)
    (stay,) = tick((stay,), (red_b,))
    if direct:
        keep_a = qkv_grad_call(meta, normed, stay, n, 2)
    else:
        keep_a = split_columns([(normed, stay[t]) for t in range(3)], core)
    red_a.keep = keep_a
    (stay,) = tick((after(stay, keep_a),), (red_a,))
    grad_hidden, extra = in_back_call(
        meta,
        stay,
        away,
        hidden,
        d_middle,
        ext,
        (found_stay, found_away),
        grad_gain_f,
        chunk_a,
    )
    (extra,) = tick((extra,), (red_b, red_a))
    extra = sum_all(ring, extra)
    sum_c = red_c.finish()
    sum_b = red_b.finish()
    sum_a = red_a.finish()
    sum_o, sum_b = sum_b[:, :h], sum_b[:, h:]
    own = [sum_a, sum_o, sum_b, sum_c]
    other = [shift(s, ring.swap_core()) for s in own]
    low = [jnp.where(core == 0, a, b) for a, b in zip(own, other)]
    high = [jnp.where(core == 0, b, a) for a, b in zip(own, other)]
    grads = [
        jnp.concatenate([low[0][:, t * h : (t + 1) * h], high[0][:, t * h : (t + 1) * h]], axis=1)
        for t in range(3)
    ]
    grad_output = jnp.concatenate([low[1], high[1]], axis=1)
    grad_inner = jnp.concatenate([low[2], high[2]], axis=1)
    grad_outer = jnp.concatenate([low[3], high[3]], axis=0)
    per = d // n
    gain_a = lax.dynamic_slice_in_dim(extra[: d // 128].reshape(-1), me * per, per, 0)
    gain_f = lax.dynamic_slice_in_dim(
        extra[d // 128 : 2 * (d // 128)].reshape(-1), me * per, per, 0
    )
    table = extra[16 : 16 + H, :BUCKETS].T.reshape(-1)
    table = lax.dynamic_slice_in_dim(table, me * rel_table.shape[0], rel_table.shape[0], 0)
    return (
        result,
        grad_hidden,
        gain_a,
        table,
        grads[0],
        grads[1],
        grads[2],
        grad_output,
        gain_f,
        grad_inner,
        grad_outer,
    )


def solution(mesh):
    both = P(("dp", "fsdp"), None)
    line = P("fsdp")
    wide = P("fsdp", None)
    in_specs = (both, line, line, wide, wide, wide, wide, line, wide, wide, P(("dp", "fsdp")), both)
    out_specs = (both, both, line, line, wide, wide, wide, wide, line, wide, wide)
    return jax.shard_map(
        functools.partial(local, Ring(mesh), Ring(mesh, split=True)),
        mesh=mesh,
        in_specs=in_specs,
        out_specs=out_specs,
        check_vma=False,
    )
```

time: 369 us -> 291 us (0.79)
  Pallas kernels: 169 us -> 129 us
  waiting for transfers between devices: 116 us -> 90.8 us
  other arithmetic: 31.5 us -> 19.9 us
  starting transfers between devices: 42 us -> 36.4 us
    pallas_call x11 -> x13, Pallas kernels: 169 us -> 129 us  [call(): pl.pallas_call(body, in_specs=[pl.BlockSpec(memory_space=pltpu.SMEM)] + [...]
    ppermute x42, waiting for transfers between devices: 116 us -> 90.8 us  [shift(): return lax.ppermute(value, ('dp', 'fsdp'), pairs)]
    convert_element_type x16 -> x12, other arithmetic: 11.4 us -> 5.19 us  [the longest x11 5.07 us: step(): self.away = add(slice(half, None)).astype(BF16)]
    ppermute x42, starting transfers between devices: 42 us -> 36.4 us  [shift(): return lax.ppermute(value, ('dp', 'fsdp'), pairs)]
    concatenate x9 -> x10, other arithmetic: 6.18 us -> 1.73 us  [the longest x9 1.72 us: join(): self.held = jnp.concatenate([self.held, got], axis=0)]
    unnamed x38 -> x32, local copies, waits for them, and re-layouts: 1.53 us -> 5.5 us
  transfers between devices with their start and end apart: 42 -> 42, of which waited for: 21 -> 25; matrix products, arithmetic and copies ran while one was open for 9% -> 5% of each run, Pallas kernels for 23% -> 45%
where the time goes in v2:
time: 291 us; the launch traced here: 288 us
  Pallas kernels  129 us (44%)
  waiting for transfers between devices  90.8 us (31%)
  starting transfers between devices  36.4 us (13%)
  other arithmetic  19.9 us (7%)
  local copies, waits for them, and re-layouts  10.3 us (4%)
    pallas_call x13, Pallas kernels, call(): pl.pallas_call(body, in_specs=[pl.BlockSpec(memory_space=pltpu.SMEM)] + [...  129 us
    ppermute x42, waiting for transfers between devices, shift(): return lax.ppermute(value, ('dp', 'fsdp'), pairs)  90.8 us
    ppermute x42, starting transfers between devices, shift(): return lax.ppermute(value, ('dp', 'fsdp'), pairs)  36.4 us
  transfers between devices with their start and end apart: 42, of which 25 were waited for; matrix products, arithmetic and copies ran while one was open for 5% of the time, Pallas kernels for 45%

profile of v2, /device:TPU:0, one launch (start us, length us, event | category | flops | bytes accessed | tf_op | source)
XLA Modules:
  0.0 287.6 jit_solution(17835667587372786237)
XLA Ops:
  4.8 4.1 %collective-permute-start = (bf16[1,48,1280]{2,1,0:T(8,128)(2,1)S(1)}, bf16[1,48,1280]{2,1,0:T(8,128)(2,1)S(1)}, u32[]{:S(2)}, u32[]{:S(2)}) collective-permute-start(bf16[1,48,1280]{2,1,0:T(8,128)(2,1)S(1)} %fusion.2), channel_id=1, source_target_pairs={{0,8},{1,9},{2,10},{3,11},{4,12},{5,13},{6,14},{7,15},{8,0},{9,1},... | collective-permute-start | bytes 368648 | tf_op jit(solution)/shard_map/ppermute | solution.py:126
  15.8 6.2 %collective-permute-done.1 = bf16[2,48,1280]{2,1,0:T(8,128)(2,1)S(1)} collective-permute-done((bf16[2,48,1280]{2,1,0:T(8,128)(2,1)S(1)}, bf16[2,48,1280]{2,1,0:T(8,128)(2,1)S(1)}, u32[]{:S(2)}, u32[]{:S(2)}) %collective-permute-start.1) | collective-permute-done | bytes 245792 | tf_op jit(solution)/shard_map/ppermute | solution.py:126
  26.8 7.9 %collective-permute-done.3 = bf16[1,48,1920]{2,1,0:T(8,128)(2,1)S(1)} collective-permute-done((bf16[1,48,1920]{2,1,0:T(8,128)(2,1)S(1)}, bf16[1,48,1920]{2,1,0:T(8,128)(2,1)S(1)}, u32[]{:S(2)}, u32[]{:S(2)}) %collective-permute-start.3) | collective-permute-done | bytes 184352 | tf_op jit(solution)/shard_map/ppermute | solution.py:126
  36.6 9.8 %collective-permute-done.5 = bf16[2,48,1920]{2,1,0:T(8,128)(2,1)S(1)} collective-permute-done((bf16[2,48,1920]{2,1,0:T(8,128)(2,1)S(1)}, bf16[2,48,1920]{2,1,0:T(8,128)(2,1)S(1)}, u32[]{:S(2)}, u32[]{:S(2)}) %collective-permute-start.5) | collective-permute-done | bytes 368672 | tf_op jit(solution)/shard_map/ppermute | solution.py:126
  50.7 4.6 %collective-permute-done.9 = bf16[1,96,768]{2,1,0:T(8,128)(2,1)S(1)} collective-permute-done((bf16[1,96,768]{2,1,0:T(8,128)(2,1)S(1)}, bf16[1,96,768]{2,1,0:T(8,128)(2,1)S(1)}, u32[]{:S(2)}, u32[]{:S(2)}) %collective-permute-start.9) | collective-permute-done | bytes 147488 | tf_op jit(solution)/shard_map/ppermute | solution.py:126
  59.1 7.3 %qkv.1 = (bf16[1024,2304]{1,0:T(8,128)(2,1)S(1)}, bf16[1024,768]{1,0:T(8,128)(2,1)S(1)}, f32[16,1024]{1,0:T(8,128)S(1)}) custom-call(s32[65]{0:T(128)S(1)} %concatenate.67.meta, bf16[1024,768]{1,0:T(8,128)(2,1)S(1)} %copy-done.2, f32[32,128]{1,0:T(8,128)S(1)} %add.206.ext_ref, bf16[8,48,1280]{2,1,0:T(8,128)(2,1)S(1)} %pad_maximum_fusion.2.rest_0_.rest_3_, ...), custom_call_target="tpu_custom_call" | custom-call | flops 3623878656 | bytes 11878400 | tf_op jit(solution)/shard_map/qkv/pallas_call | solution.py:389
  66.4 6.3 %collective-permute-done.10 = bf16[2,96,768]{2,1,0:T(8,128)(2,1)S(1)} collective-permute-done((bf16[2,96,768]{2,1,0:T(8,128)(2,1)S(1)}, bf16[2,96,768]{2,1,0:T(8,128)(2,1)S(1)}, u32[]{:S(2)}, u32[]{:S(2)}) %collective-permute-start.10) | collective-permute-done | bytes 294944 | tf_op jit(solution)/shard_map/ppermute | solution.py:126
  74.5 9.3 %attend.2 = (bf16[1024,384]{1,0:T(8,128)(2,1)S(1)}, f32[6,1024]{1,0:T(8,128)S(1)}) custom-call(s32[65]{0:T(128)S(1)} %concatenate.67.meta, bf16[1024,2304]{1,0:T(8,128)(2,1)S(1)} %get-tuple-element.114.qkv_ref, bf16[1024,128]{1,0:T(8,128)(2,1)S(1)} %get-tuple-element.235.qaug_ref, bf16[1024,128]{1,0:T(8,128)(2,1)S(1)} %get-tuple-element.234.kaug_ref, ...), custom_call_target="tpu_custom_call" | custom-call | flops 1075200000 | bytes 6119424 | tf_op jit(solution)/shard_map/attend/pallas_call | solution.py:389
  83.7 9.6 %attend.3 = (bf16[1024,384]{1,0:T(8,128)(2,1)S(1)}, f32[6,1024]{1,0:T(8,128)S(1)}) custom-call(s32[65]{0:T(128)S(1)} %concatenate.67.meta, bf16[1024,2304]{1,0:T(8,128)(2,1)S(1)} %get-tuple-element.114.qkv_ref, bf16[1024,128]{1,0:T(8,128)(2,1)S(1)} %get-tuple-element.235.qaug_ref, bf16[1024,128]{1,0:T(8,128)(2,1)S(1)} %get-tuple-element.234.kaug_ref, ...), custom_call_target="tpu_custom_call" | custom-call | flops 1075200000 | bytes 6119424 | tf_op jit(solution)/shard_map/attend/pallas_call | solution.py:389
  99.0 15.0 %mid.1 = (f32[1024,768]{1,0:T(8,128)S(1)}, bf16[1024,768]{1,0:T(8,128)(2,1)S(1)}, bf16[1024,3072]{1,0:T(8,128)(2,1)S(1)}, bf16[1024,3072]{1,0:T(8,128)(2,1)S(1)}) custom-call(s32[65]{0:T(128)S(1)} %concatenate.67.meta, bf16[1024,384]{1,0:T(8,128)(2,1)S(1)} %get-tuple-element.116.low_ref, bf16[1024,384]{1,0:T(8,128)(2,1)S(1)} %get-tuple-element.122.high_ref, ...), custom_call_target="tpu_custom_call" | custom-call | flops 6039797760 | bytes 26361856 | tf_op jit(solution)/shard_map/mid/pallas_call | solution.py:389
  115.2 6.0 %outer_grad.1 = (bf16[16,96,768]{2,1,0:T(8,128)(2,1)S(1)}, bf16[16,96,768]{2,1,0:T(8,128)(2,1)S(1)}) custom-call(s32[65]{0:T(128)S(1)} %concatenate.67.meta, bf16[1024,3072]{1,0:T(8,128)(2,1)S(1)} %get-tuple-element.128.act_ref, bf16[1024,768]{1,0:T(8,128)(2,1)S(1)} %copy-done.3), custom_call_target="tpu_custom_call" | custom-call | flops 4831838208 | bytes 12582912 | tf_op jit(solution)/shard_map/outer_grad/pallas_call | solution.py:389
  121.9 5.6 %collective-permute-done.16.rest_2_ = bf16[8,96,768]{2,1,0:T(8,128)(2,1)S(1)} collective-permute-done((bf16[8,96,768]{2,1,0:T(8,128)(2,1)S(1)}, bf16[8,96,768]{2,1,0:T(8,128)(2,1)S(1)}, u32[]{:S(2)}, u32[]{:S(2)}) %collective-permute-start.16) | collective-permute-done | bytes 1179680 | tf_op jit(solution)/shard_map/ppermute | solution.py:126
  132.0 20.1 %out.1 = (f32[1024,768]{1,0:T(8,128)}, bf16[1024,3072]{1,0:T(8,128)(2,1)S(1)}) custom-call(s32[65]{0:T(128)S(1)} %concatenate.66.meta, bf16[1024,3072]{1,0:T(8,128)(2,1)S(1)} %copy-done.9, f32[1024,768]{1,0:T(8,128)S(1)} %get-tuple-element.129.mid_ref, bf16[1024,768]{1,0:T(8,128)(2,1)S(1)} %copy-done.3, ...), custom_call_target="tpu_custom_call", output_to_operand_aliasing={{1}: (4, {})} | custom-call | flops 9663676416 | bytes 31457280 | tf_op jit(solution)/shard_map/out/pallas_call | solution.py:389
  156.5 13.9 %mid_back.1 = (f32[1024,768]{1,0:T(8,128)S(1)}, bf16[1024,768]{1,0:T(8,128)(2,1)S(1)}, bf16[1024,768]{1,0:T(8,128)(2,1)S(1)}, f32[1,768]{1,0:T(1,128)S(1)}) custom-call(s32[65]{0:T(128)S(1)} %concatenate.67.meta, bf16[1024,3072]{1,0:T(8,128)(2,1)S(1)} %get-tuple-element.138.din_ref, f32[1024,768]{1,0:T(8,128)S(1)} %copy-done.7, ...), custom_call_target="tpu_custom_call" | custom-call | flops 6039797760 | bytes 23219200 | tf_op jit(solution)/shard_map/mid_back/pallas_call | solution.py:389
  174.1 7.7 %mid_grad.1 = (bf16[16,48,1920]{2,1,0:T(8,128)(2,1)S(1)}, bf16[16,48,1920]{2,1,0:T(8,128)(2,1)S(1)}) custom-call(s32[65]{0:T(128)S(1)} %concatenate.67.meta, bf16[1024,768]{1,0:T(8,128)(2,1)S(1)} %copy-done.11, bf16[1024,384]{1,0:T(8,128)(2,1)S(1)} %get-tuple-element.116.low_ref, bf16[1024,384]{1,0:T(8,128)(2,1)S(1)} %get-tuple-element.122.high_ref, ...), custom_call_target="tpu_custom_call" | custom-call | flops 6039797760 | bytes 16908288 | tf_op jit(solution)/shard_map/mid_grad/pallas_call | solution.py:389
  184.8 11.7 %attend_back.2 = (bf16[3,1024,384]{2,1,0:T(8,128)(2,1)S(1)}, f32[8,1024]{1,0:T(8,128)S(1)}) custom-call(s32[65]{0:T(128)S(1)} %concatenate.67.meta, bf16[1024,2304]{1,0:T(8,128)(2,1)S(1)} %get-tuple-element.114.qkv_ref, bf16[1024,768]{1,0:T(8,128)(2,1)S(1)} %get-tuple-element.164.dctx_ref, bf16[1024,128]{1,0:T(8,128)(2,1)S(1)} %get-tuple-element.235.qaug_ref, ...), custom_call_target="tpu_custom_call" | custom-call | flops 2688000000 | bytes 9322496 | tf_op jit(solution)/shard_map/attend_back/pallas_call | solution.py:389
  202.2 11.7 %attend_back.3 = (bf16[3,1024,384]{2,1,0:T(8,128)(2,1)S(1)}, f32[8,1024]{1,0:T(8,128)S(1)}) custom-call(s32[65]{0:T(128)S(1)} %concatenate.67.meta, bf16[1024,2304]{1,0:T(8,128)(2,1)S(1)} %get-tuple-element.114.qkv_ref, bf16[1024,768]{1,0:T(8,128)(2,1)S(1)} %copy-done.5, bf16[1024,128]{1,0:T(8,128)(2,1)S(1)} %get-tuple-element.235.qaug_ref, ...), custom_call_target="tpu_custom_call" | custom-call | flops 2688000000 | bytes 9322496 | tf_op jit(solution)/shard_map/attend_back/pallas_call | solution.py:389
  217.3 3.4 %qkv_grad.3 = bf16[16,48,1152]{2,1,0:T(8,128)(2,1)S(1)} custom-call(s32[65]{0:T(128)S(1)} %concatenate.67.meta, bf16[1024,768]{1,0:T(8,128)(2,1)S(1)} %get-tuple-element.153.n_ref, bf16[3,1024,384]{2,1,0:T(8,128)(2,1)S(1)} %get-tuple-element.173.d_ref.own_ref), custom_call_target="tpu_custom_call" | custom-call | flops 1811939328 | bytes 5701632 | tf_op jit(solution)/shard_map/qkv_grad/pallas_call | solution.py:389
  223.5 10.0 %in_back.1 = (f32[1024,768]{1,0:T(8,128)}, f32[32,128]{1,0:T(8,128)S(1)}) custom-call(s32[65]{0:T(128)S(1)} %concatenate.67.meta, bf16[3,1024,384]{2,1,0:T(8,128)(2,1)S(1)} %get-tuple-element.173.d_ref.own_ref, bf16[3,1024,384]{2,1,0:T(8,128)(2,1)S(1)} %get-tuple-element.163.d_ref.rec_ref, bf16[1024,768]{1,0:T(8,128)(2,1)S(1)} %copy-done.2, ...), custom_call_target="tpu_custom_call" | custom-call | flops 3623878656 | bytes 16616448 | tf_op jit(solution)/shard_map/in_back/pallas_call | solution.py:389
  233.5 6.7 %collective-permute-done.25 = bf16[4,48,1920]{2,1,0:T(8,128)(2,1)S(1)} collective-permute-done((bf16[4,48,1920]{2,1,0:T(8,128)(2,1)S(1)}, bf16[4,48,1920]{2,1,0:T(8,128)(2,1)S(1)}, u32[]{:S(2)}, u32[]{:S(2)}) %collective-permute-start.25) | collective-permute-done | bytes 737312 | tf_op jit(solution)/shard_map/ppermute | solution.py:126
  242.7 3.8 %collective-permute-done.28 = f32[32,128]{1,0:T(8,128)S(1)} collective-permute-done((f32[32,128]{1,0:T(8,128)S(1)}, f32[32,128]{1,0:T(8,128)S(1)}, u32[]{:S(2)}, u32[]{:S(2)}) %collective-permute-start.28) | collective-permute-done | bytes 16416 | tf_op jit(solution)/shard_map/ppermute | solution.py:126
  261.1 6.5 %collective-permute-done.37 = bf16[1,48,1920]{2,1,0:T(8,128)(2,1)S(1)} collective-permute-done((bf16[1,48,1920]{2,1,0:T(8,128)(2,1)S(1)}, bf16[1,48,1920]{2,1,0:T(8,128)(2,1)S(1)}, u32[]{:S(2)}, u32[]{:S(2)}) %collective-permute-start.37) | collective-permute-done | bytes 184352 | tf_op jit(solution)/shard_map/ppermute | solution.py:126
  268.9 6.7 %collective-permute-done.33 = bf16[2,48,1152]{2,1,0:T(8,128)(2,1)S(1)} collective-permute-done((bf16[2,48,1152]{2,1,0:T(8,128)(2,1)S(1)}, bf16[2,48,1152]{2,1,0:T(8,128)(2,1)S(1)}, u32[]{:S(2)}, u32[]{:S(2)}) %collective-permute-start.33) | collective-permute-done | bytes 221216 | tf_op jit(solution)/shard_map/ppermute | solution.py:126
  277.1 6.6 %collective-permute-done.34 = bf16[1,48,1152]{2,1,0:T(8,128)(2,1)S(1)} collective-permute-done((bf16[1,48,1152]{2,1,0:T(8,128)(2,1)S(1)}, bf16[1,48,1152]{2,1,0:T(8,128)(2,1)S(1)}, u32[]{:S(2)}, u32[]{:S(2)}) %collective-permute-start.34) | collective-permute-done | bytes 110624 | tf_op jit(solution)/shard_map/ppermute | solution.py:126
  (194 shorter events, 85.8 us)
Async XLA Ops:
  4.8 10.1 %collective-permute-start = (bf16[1,48,1280]{2,1,0:T(8,128)(2,1)S(1)}, bf16[1,48,1280]{2,1,0:T(8,128)(2,1)S(1)}, u32[]{:S(2)}, u32[]{:S(2)}) collective-permute-start(bf16[1,48,1280]{2,1,0:T(8,128)(2,1)S(1)} %fusion.2), channel_id=1, source_target_pairs={{0,8},{1,9},{2,10},{3,11},{4,12},{5,13},{6,14},{7,15},{8,0},{9,1},... | collective-permute-start | bytes 368648 | tf_op jit(solution)/shard_map/ppermute | solution.py:126
  22.1 12.7 %collective-permute-start.2 = (bf16[4,48,1280]{2,1,0:T(8,128)(2,1)S(1)}, bf16[4,48,1280]{2,1,0:T(8,128)(2,1)S(1)}, u32[]{:S(2)}, u32[]{:S(2)}) collective-permute-start(bf16[4,48,1280]{2,1,0:T(8,128)(2,1)S(1)} %pad_maximum_fusion.7), channel_id=1, source_target_pairs={{0,2},{1,3},{2,0},{3,1},{4,6},{5,7},{6,4},{7,5},{8,10},{9,11},{10,... | collective-permute-start | bytes 1474568 | tf_op jit(solution)/shard_map/ppermute | solution.py:126
  23.4 11.3 %collective-permute-start.3 = (bf16[1,48,1920]{2,1,0:T(8,128)(2,1)S(1)}, bf16[1,48,1920]{2,1,0:T(8,128)(2,1)S(1)}, u32[]{:S(2)}, u32[]{:S(2)}) collective-permute-start(bf16[1,48,1920]{2,1,0:T(8,128)(2,1)S(1)} %maximum_bitcast_fusion), channel_id=1, source_target_pairs={{0,8},{1,9},{2,10},{3,11},{4,12},{5,13},{6,14},{7,15},{8,0},{9,1},... | collective-permute-start | bytes 552968 | tf_op jit(solution)/shard_map/ppermute | solution.py:126
  34.9 14.3 %collective-permute-start.4 = (bf16[8,48,1280]{2,1,0:T(8,128)(2,1)S(1)}, bf16[8,48,1280]{2,1,0:T(8,128)(2,1)}, u32[]{:S(2)}, u32[]{:S(2)}) collective-permute-start(bf16[8,48,1280]{2,1,0:T(8,128)(2,1)S(1)} %pad_maximum_fusion.2.rest_0_.rest_3_), channel_id=1, source_target_pairs={{0,1},{1,0},{2,3},{3,2},{4,5},{5,4},{6,7},{7,6},{8,9},{9,8},{10,11... | collective-permute-start | bytes 2949128 | tf_op jit(solution)/shard_map/ppermute | solution.py:126
  35.5 10.9 %collective-permute-start.5 = (bf16[2,48,1920]{2,1,0:T(8,128)(2,1)S(1)}, bf16[2,48,1920]{2,1,0:T(8,128)(2,1)S(1)}, u32[]{:S(2)}, u32[]{:S(2)}) collective-permute-start(bf16[2,48,1920]{2,1,0:T(8,128)(2,1)S(1)} %pad_maximum_fusion.8), channel_id=1, source_target_pairs={{0,4},{1,5},{2,6},{3,7},{4,0},{5,1},{6,2},{7,3},{8,12},{9,13},{10,... | collective-permute-start | bytes 1105928 | tf_op jit(solution)/shard_map/ppermute | solution.py:126
  36.2 22.9 %collective-permute-start.6 = (bf16[8,48,1280]{2,1,0:T(8,128)(2,1)S(1)}, bf16[8,48,1280]{2,1,0:T(8,128)(2,1)}, u32[]{:S(2)}, u32[]{:S(2)}) collective-permute-start(bf16[8,48,1280]{2,1,0:T(8,128)(2,1)S(1)} %pad_maximum_fusion.2.rest_0_.rest_3_), channel_id=1, source_target_pairs={{0,16},{1,17},{2,18},{3,19},{4,20},{5,21},{6,22},{7,23},{8,24},{9,... | collective-permute-start | bytes 2949128 | tf_op jit(solution)/shard_map/ppermute | solution.py:126
  56.5 16.3 %collective-permute-start.8 = (bf16[4,48,1920]{2,1,0:T(8,128)(2,1)S(1)}, bf16[4,48,1920]{2,1,0:T(8,128)(2,1)S(1)}, u32[]{:S(2)}, u32[]{:S(2)}) collective-permute-start(bf16[4,48,1920]{2,1,0:T(8,128)(2,1)S(1)} %pad_maximum_fusion.3), channel_id=1, source_target_pairs={{0,2},{1,3},{2,0},{3,1},{4,6},{5,7},{6,4},{7,5},{8,10},{9,11},{10,... | collective-permute-start | bytes 2211848 | tf_op jit(solution)/shard_map/ppermute | solution.py:126
  58.1 14.6 %collective-permute-start.10 = (bf16[2,96,768]{2,1,0:T(8,128)(2,1)S(1)}, bf16[2,96,768]{2,1,0:T(8,128)(2,1)S(1)}, u32[]{:S(2)}, u32[]{:S(2)}) collective-permute-start(bf16[2,96,768]{2,1,0:T(8,128)(2,1)S(1)} %pad_maximum_fusion.9), channel_id=1, source_target_pairs={{0,8},{1,9},{2,10},{3,11},{4,12},{5,13},{6,14},{7,15},{8,0},{9,1},... | collective-permute-start | bytes 884744 | tf_op jit(solution)/shard_map/ppermute | solution.py:126
  72.9 20.6 %collective-permute-start.11 = (bf16[8,48,1920]{2,1,0:T(8,128)(2,1)S(1)}, bf16[8,48,1920]{2,1,0:T(8,128)(2,1)S(1)}, u32[]{:S(2)}, u32[]{:S(2)}) collective-permute-start(bf16[8,48,1920]{2,1,0:T(8,128)(2,1)S(1)} %pad_maximum_fusion.rest_0_), channel_id=1, source_target_pairs={{0,1},{1,0},{2,3},{3,2},{4,5},{5,4},{6,7},{7,6},{8,9},{9,8},{10,11... | collective-permute-start | bytes 4423688 | tf_op jit(solution)/shard_map/ppermute | solution.py:126
  74.5 18.9 %collective-permute-start.12 = (bf16[4,96,768]{2,1,0:T(8,128)(2,1)S(1)}, bf16[4,96,768]{2,1,0:T(8,128)(2,1)S(1)}, u32[]{:S(2)}, u32[]{:S(2)}) collective-permute-start(bf16[4,96,768]{2,1,0:T(8,128)(2,1)S(1)} %pad_maximum_fusion.4), channel_id=1, source_target_pairs={{0,4},{1,5},{2,6},{3,7},{4,0},{5,1},{6,2},{7,3},{8,12},{9,13},{10,... | collective-permute-start | bytes 1769480 | tf_op jit(solution)/shard_map/ppermute | solution.py:126
  94.1 27.7 %collective-permute-start.15 = (bf16[8,96,768]{2,1,0:T(8,128)(2,1)S(1)}, bf16[8,96,768]{2,1,0:T(8,128)(2,1)S(1)}, u32[]{:S(2)}, u32[]{:S(2)}) collective-permute-start(bf16[8,96,768]{2,1,0:T(8,128)(2,1)S(1)} %pad_maximum_fusion.1.rest_0_), channel_id=1, source_target_pairs={{0,2},{1,3},{2,0},{3,1},{4,6},{5,7},{6,4},{7,5},{8,10},{9,11},{10,... | collective-permute-start | bytes 3538952 | tf_op jit(solution)/shard_map/ppermute | solution.py:126
  121.2 30.8 %collective-permute-start.18 = (bf16[16,96,768]{2,1,0:T(8,128)(2,1)S(1)}, bf16[16,96,768]{2,1,0:T(8,128)(2,1)S(1)}, u32[]{:S(2)}, u32[]{:S(2)}) collective-permute-start(bf16[16,96,768]{2,1,0:T(8,128)(2,1)S(1)} %get-tuple-element.136), channel_id=1, source_target_pairs={{0,16},{1,17},{2,18},{3,19},{4,20},{5,21},{6,22},{7,23},{8,24},{9,... | collective-permute-start | bytes 7077896 | tf_op jit(solution)/shard_map/ppermute | solution.py:126
  155.9 16.3 %collective-permute-start.19 = (bf16[8,96,768]{2,1,0:T(8,128)(2,1)S(1)}, bf16[8,96,768]{2,1,0:T(8,128)(2,1)S(1)}, u32[]{:S(2)}, u32[]{:S(2)}) collective-permute-start(bf16[8,96,768]{2,1,0:T(8,128)(2,1)S(1)} %get-tuple-element.143), channel_id=1, source_target_pairs={{0,1},{1,0},{2,3},{3,2},{4,5},{5,4},{6,7},{7,6},{8,9},{9,8},{10,11... | collective-permute-start | bytes 3538952 | tf_op jit(solution)/shard_map/ppermute | solution.py:126
  182.6 14.0 %collective-permute-start.22 = (bf16[16,48,1920]{2,1,0:T(8,128)(2,1)S(1)}, bf16[16,48,1920]{2,1,0:T(8,128)(2,1)S(1)}, u32[]{:S(2)}, u32[]{:S(2)}) collective-permute-start(bf16[16,48,1920]{2,1,0:T(8,128)(2,1)S(1)} %get-tuple-element.161), channel_id=1, source_target_pairs={{0,16},{1,17},{2,18},{3,19},{4,20},{5,21},{6,22},{7,23},{8,24},{9,... | collective-permute-start | bytes 8847368 | tf_op jit(solution)/shard_map/ppermute | solution.py:126
  182.7 13.8 %collective-permute-start.21 = (bf16[2,96,768]{2,1,0:T(8,128)(2,1)S(1)}, bf16[2,96,768]{2,1,0:T(8,128)(2,1)S(1)}, u32[]{:S(2)}, u32[]{:S(2)}) collective-permute-start(bf16[2,96,768]{2,1,0:T(8,128)(2,1)S(1)} %get-tuple-element.158), channel_id=1, source_target_pairs={{0,4},{1,5},{2,6},{3,7},{4,0},{5,1},{6,2},{7,3},{8,12},{9,13},{10,... | collective-permute-start | bytes 884744 | tf_op jit(solution)/shard_map/ppermute | solution.py:126
  197.3 19.6 %collective-permute-start.23 = (bf16[8,48,1920]{2,1,0:T(8,128)(2,1)S(1)}, bf16[8,48,1920]{2,1,0:T(8,128)(2,1)S(1)}, u32[]{:S(2)}, u32[]{:S(2)}) collective-permute-start(bf16[8,48,1920]{2,1,0:T(8,128)(2,1)S(1)} %get-tuple-element.167), channel_id=1, source_target_pairs={{0,1},{1,0},{2,3},{3,2},{4,5},{5,4},{6,7},{7,6},{8,9},{9,8},{10,11... | collective-permute-start | bytes 4423688 | tf_op jit(solution)/shard_map/ppermute | solution.py:126
  201.3 21.1 %collective-permute-start.24 = (bf16[16,48,1152]{2,1,0:T(8,128)(2,1)S(1)}, bf16[16,48,1152]{2,1,0:T(8,128)(2,1)S(1)}, u32[]{:S(2)}, u32[]{:S(2)}) collective-permute-start(bf16[16,48,1152]{2,1,0:T(8,128)(2,1)S(1)} %qkv_grad.2), channel_id=1, source_target_pairs={{0,16},{1,17},{2,18},{3,19},{4,20},{5,21},{6,22},{7,23},{8,24},{9,... | collective-permute-start | bytes 5308424 | tf_op jit(solution)/shard_map/ppermute | solution.py:126
  202.2 21.2 %collective-permute-start.40 = (bf16[1,96,768]{2,1,0:T(8,128)(2,1)S(1)}, bf16[1,96,768]{2,1,0:T(8,128)(2,1)S(1)}, u32[]{:S(2)}, u32[]{:S(2)}) collective-permute-start(bf16[1,96,768]{2,1,0:T(8,128)(2,1)S(1)} %get-tuple-element.192), channel_id=1, source_target_pairs={{0,8},{1,9},{2,10},{3,11},{4,12},{5,13},{6,14},{7,15},{8,0},{9,1},... | collective-permute-start | bytes 442376 | tf_op jit(solution)/shard_map/ppermute | solution.py:126
  220.7 19.4 %collective-permute-start.25 = (bf16[4,48,1920]{2,1,0:T(8,128)(2,1)S(1)}, bf16[4,48,1920]{2,1,0:T(8,128)(2,1)S(1)}, u32[]{:S(2)}, u32[]{:S(2)}) collective-permute-start(bf16[4,48,1920]{2,1,0:T(8,128)(2,1)S(1)} %get-tuple-element.181), channel_id=1, source_target_pairs={{0,2},{1,3},{2,0},{3,1},{4,6},{5,7},{6,4},{7,5},{8,10},{9,11},{10,... | collective-permute-start | bytes 2211848 | tf_op jit(solution)/shard_map/ppermute | solution.py:126
  222.8 17.5 %collective-permute-start.26 = (bf16[8,48,1152]{2,1,0:T(8,128)(2,1)S(1)}, bf16[8,48,1152]{2,1,0:T(8,128)(2,1)S(1)}, u32[]{:S(2)}, u32[]{:S(2)}) collective-permute-start(bf16[8,48,1152]{2,1,0:T(8,128)(2,1)S(1)} %get-tuple-element.184), channel_id=1, source_target_pairs={{0,1},{1,0},{2,3},{3,2},{4,5},{5,4},{6,7},{7,6},{8,9},{9,8},{10,11... | collective-permute-start | bytes 2654216 | tf_op jit(solution)/shard_map/ppermute | solution.py:126
  223.4 28.5 %collective-permute-start.41 = (f32[96,768]{1,0:T(8,128)S(1)}, f32[96,768]{1,0:T(8,128)S(1)}, u32[]{:S(2)}, u32[]{:S(2)}) collective-permute-start(f32[96,768]{1,0:T(8,128)S(1)} %add_bitcast_fusion.1), channel_id=1, source_target_pairs={{0,16},{1,17},{2,18},{3,19},{4,20},{5,21},{6,22},{7,23},{8,24},{9,... | collective-permute-start | bytes 884744 | tf_op jit(solution)/shard_map/ppermute | solution.py:126
  246.7 12.6 %collective-permute-start.36 = (bf16[2,48,1920]{2,1,0:T(8,128)(2,1)S(1)}, bf16[2,48,1920]{2,1,0:T(8,128)(2,1)S(1)}, u32[]{:S(2)}, u32[]{:S(2)}) collective-permute-start(bf16[2,48,1920]{2,1,0:T(8,128)(2,1)S(1)} %get-tuple-element.190), channel_id=1, source_target_pairs={{0,4},{1,5},{2,6},{3,7},{4,0},{5,1},{6,2},{7,3},{8,12},{9,13},{10,... | collective-permute-start | bytes 1105928 | tf_op jit(solution)/shard_map/ppermute | solution.py:126
  256.4 11.2 %collective-permute-start.32 = (bf16[4,48,1152]{2,1,0:T(8,128)(2,1)S(1)}, bf16[4,48,1152]{2,1,0:T(8,128)(2,1)S(1)}, u32[]{:S(2)}, u32[]{:S(2)}) collective-permute-start(bf16[4,48,1152]{2,1,0:T(8,128)(2,1)S(1)} %get-tuple-element.188), channel_id=1, source_target_pairs={{0,2},{1,3},{2,0},{3,1},{4,6},{5,7},{6,4},{7,5},{8,10},{9,11},{10,... | collective-permute-start | bytes 1327112 | tf_op jit(solution)/shard_map/ppermute | solution.py:126
  267.9 15.9 %collective-permute-start.39 = (f32[48,1536]{1,0:T(8,128)S(1)}, f32[48,1536]{1,0:T(8,128)S(1)}, u32[]{:S(2)}, u32[]{:S(2)}) collective-permute-start(f32[48,1536]{1,0:T(8,128)S(1)} %slice.268), channel_id=1, source_target_pairs={{0,16},{1,17},{2,18},{3,19},{4,20},{5,21},{6,22},{7,23},{8,24},{9,... | collective-permute-start | bytes 884744 | tf_op jit(solution)/shard_map/ppermute | solution.py:126
  (34 other events, 233.1 us)
